TPU v7x, 32 devices: a whole 2x2x4 slice. The times are simulated.
32 devices in a mesh: groups: 2 (over y), seq: 4 (over z), chan: 2 (over x), sub: 2 (over core).
Axes of the slice: x: 2, y: 2, z: 4, core: 2. Of those that a mesh axis runs over, the one named last changes fastest.
Arguments:
- features: bfloat16 [3, 4096, 2048], P(None, ('chan', 'sub'), ('groups', 'seq')), parts along dimension 2, may hold values from -6 to 6
- dout: bfloat16 [4096, 2048], P(('chan', 'sub'), ('groups', 'seq')), parts along dimension 1, may hold values from -6 to 6
- filters: bfloat16 [4096, 1024], P(('chan', 'sub'), 'seq'), may hold values from -0.1875 to 0.1875
- taps: float32 [3, 3, 4096], P(None, None, ('chan', 'sub')), may hold values from -3.5 to 3.5
- skip: float32 [4096], P(('chan', 'sub')), may hold values from -4 to 4
- lengths: int32 [32], P('groups'), parts along dimension 0, may hold values from 1 to 256, 1024 in all
Outputs:
- out: bfloat16 [4096, 2048], P(('chan', 'sub'), ('groups', 'seq')), parts along dimension 1
- dfeatures: bfloat16 [3, 4096, 2048], P(None, ('chan', 'sub'), ('groups', 'seq')), parts along dimension 2
There are 2 independent parts, one for each index of `groups`. A program takes and returns all parts, laid end to end along the dimension named above; an argument that names none is the same for every part. Nothing has to cross between parts.
Inputs may be any that keep to these rules, and one draw needn't show every extreme that they name: The lengths of one part sum to 1024, and the longest genome has exactly 256 positions.
All inputs are finite; a program needn't handle non-finite values.
Results may differ from a plain program's by a relative error of at most 0.01.
Values may be sent and summed in bfloat16 or wider, within the bound.
A program may use at most 64 MiB of HBM per device.

v0:
```python
import jax
import jax.numpy as jnp
from jax import lax
from jax.sharding import PartitionSpec as P

HIGHEST = lax.Precision.HIGHEST
TWO_PI = 6.283185307179586


def shifted(value, axis, steps):
    count = lax.axis_size(axis)
    leading, last = (max(0, -steps), min(count, count - steps))
    return lax.ppermute(value, axis, [(source, source + steps) for source in range(leading, last)])


def genome_offsets(lengths, positions):
    ends_at = jnp.cumsum(lengths, dtype=jnp.int32)
    before = (ends_at[None, :] <= positions[:, None]).astype(jnp.int32)
    return positions - jnp.sum(before * lengths[None, :], axis=1, dtype=jnp.int32)


def short_forward(extended, taps_local, offsets):
    span_rows = offsets.shape[0]
    count = taps_local.shape[1]
    result = jnp.zeros(extended.shape[:2] + (span_rows,), jnp.float32)
    for tap_index in range(count):
        begin = count - 1 - tap_index
        window = extended[:, :, begin : begin + span_rows].astype(jnp.float32)
        keep_mask = (offsets >= tap_index).astype(jnp.float32)
        result = result + taps_local[:, tap_index, :, None] * window * keep_mask[None, None, :]
    return result


def short_backward(grads_ext, taps_local, offsets_ext):
    count = taps_local.shape[1]
    span_rows = offsets_ext.shape[0] - (count - 1)
    result = jnp.zeros(grads_ext.shape[:2] + (span_rows,), jnp.float32)
    for tap_index in range(count):
        window = grads_ext[:, :, tap_index : tap_index + span_rows]
        keep_mask = (offsets_ext[tap_index : tap_index + span_rows] >= tap_index).astype(
            jnp.float32
        )
        result = result + taps_local[:, tap_index, :, None] * window * keep_mask[None, None, :]
    return result


def dft_table(rows_n, cols_n, period):
    row_ids = jnp.arange(rows_n, dtype=jnp.int32)
    col_ids = jnp.arange(cols_n, dtype=jnp.int32)
    phase = row_ids[:, None] * col_ids[None, :] % period
    angles = phase.astype(jnp.float32) * (-TWO_PI / period)
    return (jnp.cos(angles), jnp.sin(angles))


def forward_transform(signal, tables):
    (row_re, row_im), (twid_re, twid_im), (col_re, col_im) = tables
    half_rows = signal.shape[1] // 128
    blocks_in = signal.reshape(signal.shape[0], half_rows, 128)
    part_re = jnp.einsum("kn,cnm->ckm", row_re[:, :half_rows], blocks_in, precision=HIGHEST)
    part_im = jnp.einsum("kn,cnm->ckm", row_im[:, :half_rows], blocks_in, precision=HIGHEST)
    turned_re = part_re * twid_re - part_im * twid_im
    turned_im = part_re * twid_im + part_im * twid_re
    spec_re = jnp.einsum("ckn,nm->ckm", turned_re, col_re, precision=HIGHEST) - jnp.einsum(
        "ckn,nm->ckm", turned_im, col_im, precision=HIGHEST
    )
    spec_im = jnp.einsum("ckn,nm->ckm", turned_re, col_im, precision=HIGHEST) + jnp.einsum(
        "ckn,nm->ckm", turned_im, col_re, precision=HIGHEST
    )
    return (spec_re, spec_im)


def inverse_transform(spec_re, spec_im, tables):
    (row_re, row_im), (twid_re, twid_im), (col_re, col_im) = tables
    rows_n = spec_re.shape[1]
    half_rows = rows_n // 2
    mid_re = jnp.einsum("ckn,nm->ckm", spec_re, col_re, precision=HIGHEST) + jnp.einsum(
        "ckn,nm->ckm", spec_im, col_im, precision=HIGHEST
    )
    mid_im = jnp.einsum("ckn,nm->ckm", spec_im, col_re, precision=HIGHEST) - jnp.einsum(
        "ckn,nm->ckm", spec_re, col_im, precision=HIGHEST
    )
    back_re = mid_re * twid_re + mid_im * twid_im
    back_im = mid_im * twid_re - mid_re * twid_im
    signal = jnp.einsum("nk,ckm->cnm", row_re[:half_rows], back_re, precision=HIGHEST) + jnp.einsum(
        "nk,ckm->cnm", row_im[:half_rows], back_im, precision=HIGHEST
    )
    return signal.reshape(signal.shape[0], half_rows * 128) * (1.0 / (rows_n * 128))


def long_filter(filt, mixed_in, grad_in, skip_part):
    rows_n = 2 * mixed_in.shape[1] // 128
    tables = (
        dft_table(rows_n, rows_n, rows_n),
        dft_table(rows_n, 128, rows_n * 128),
        dft_table(128, 128, 128),
    )
    mixed_f = mixed_in.astype(jnp.float32)
    grad_f = grad_in.astype(jnp.float32)
    filt_re, filt_im = forward_transform(filt.astype(jnp.float32), tables)
    mix_re, mix_im = forward_transform(mixed_f, tables)
    grad_re, grad_im = forward_transform(grad_f, tables)
    conv_out = inverse_transform(
        filt_re * mix_re - filt_im * mix_im, filt_re * mix_im + filt_im * mix_re, tables
    )
    corr_out = inverse_transform(
        filt_re * grad_re + filt_im * grad_im, filt_re * grad_im - filt_im * grad_re, tables
    )
    y_out = (conv_out + skip_part[:, None] * mixed_f).astype(jnp.bfloat16)
    dmixed = (corr_out + skip_part[:, None] * grad_f).astype(jnp.bfloat16)
    return (y_out, dmixed)


def to_channels(stacked):
    return lax.all_to_all(stacked, "seq", split_axis=1, concat_axis=2, tiled=True)


def to_sequence(stacked):
    return lax.all_to_all(stacked, "seq", split_axis=2, concat_axis=1, tiled=True)


def local(features, dout, filters, taps, skip, lengths):
    blocks = lax.axis_size("seq")
    seq_rank = lax.axis_index("seq")
    span_rows = features.shape[2]
    channels_here = features.shape[1]
    chan_part = channels_here // blocks
    count = taps.shape[1]
    margin = count - 1
    rim = shifted(features[:, :, span_rows - margin :], "seq", 1)
    extended = jnp.concatenate([rim, features], axis=2)
    first_pos = seq_rank * span_rows
    offsets = genome_offsets(lengths, first_pos + jnp.arange(span_rows, dtype=jnp.int32))
    filtered = short_forward(extended, taps, offsets).astype(jnp.bfloat16)
    query_side = filtered[0].astype(jnp.float32)
    key_side = filtered[1].astype(jnp.float32)
    value_side = filtered[2].astype(jnp.float32)
    dout_f = dout.astype(jnp.float32)
    mixed = (key_side * value_side).astype(jnp.bfloat16)
    grad_in = (dout_f * query_side).astype(jnp.bfloat16)
    moved = to_channels(jnp.stack([mixed, grad_in, filters]))
    skip_part = lax.dynamic_slice_in_dim(skip, seq_rank * chan_part, chan_part, 0)
    y_out, dmixed = long_filter(moved[2], moved[0], moved[1], skip_part)
    returned = to_sequence(jnp.stack([y_out, dmixed]))
    y_here = returned[0].astype(jnp.float32)
    dmixed_here = returned[1].astype(jnp.float32)
    out = (query_side * y_here).astype(jnp.bfloat16)
    grads = jnp.stack([dout_f * y_here, dmixed_here * value_side, dmixed_here * key_side])
    ahead = shifted(grads[:, :, :margin], "seq", -1)
    grads_ext = jnp.concatenate([grads, ahead], axis=2)
    offsets_ext = genome_offsets(
        lengths, first_pos + jnp.arange(span_rows + margin, dtype=jnp.int32)
    )
    dfeatures = short_backward(grads_ext, taps, offsets_ext).astype(jnp.bfloat16)
    return (out, dfeatures)


def solution(mesh):
    in_specs = (
        P(None, ("chan", "sub"), ("groups", "seq")),
        P(("chan", "sub"), ("groups", "seq")),
        P(("chan", "sub"), "seq"),
        P(None, None, ("chan", "sub")),
        P(("chan", "sub")),
        P("groups"),
    )
    out_specs = (P(("chan", "sub"), ("groups", "seq")), P(None, ("chan", "sub"), ("groups", "seq")))
    return jax.shard_map(local, mesh=mesh, in_specs=in_specs, out_specs=out_specs, check_vma=False)
```

profile of v0, /device:TPU:0, one launch (start us, length us, event | category | flops | bytes accessed | tf_op | source)
XLA Modules:
  0.0 219.7 jit_solution(16636428036014913479)
XLA Ops:
  2.5 5.0 %collective-permute-start = (bf16[3,1024,2]{1,2,0:T(2,128)(2,1)S(1)}, bf16[3,1024,2]{1,2,0:T(2,128)(2,1)S(1)}, u32[]{:S(2)}, u32[]{:S(2)}) collective-permute-start(bf16[3,1024,2]{1,2,0:T(2,128)(2,1)S(1)} %copy.272), channel_id=1, source_target_pairs={{0,4},{4,8},{8,12},{1,5},{5,9},{9,13},{2,6},{6,10},{10,14},{3,7},{... | collective-permute-start | bytes 36872 | tf_op jit(solution)/shard_map/ppermute | solution.py:13
  9.3 3.0 %add_convert_fusion = bf16[3,1024,256]{2,1,0:T(8,128)(2,1)S(1)} fusion(bf16[3,1024,256]{2,1,0:T(8,128)(2,1)S(1)} %copy-done.8, bf16[3,1024,2]{2,1,0:T(8,128)(2,1)S(1)} %copy.207, f32[256]{0:T(256)S(1)} %get-tuple-element.39, f32[3,1024]{1,0:T(4,128)S(1)} %get-tuple-element.40, f32[256]{0:T(256)S(1)} %get-tuple-element.38, ...), kind=kLoop, calls=%fused_computation.9 | loop fusion | flops 14155776 | bytes 3197952 | tf_op jit(solution)/shard_map/convert_element_type | solution.py:133
  13.9 2.7 %copy.208 = bf16[3,1024,256]{2,0,1:T(4,128)(2,1)} copy(bf16[3,1024,256]{2,1,0:T(8,128)(2,1)S(1)} %pad_maximum_fusion.3) | data formatting | bytes 3145728 | tf_op jit(solution)/shard_map/stack | solution.py:140
  16.6 5.7 %all-to-all-start = ((bf16[3,1024,256]{2,0,1:T(4,128)(2,1)}), bf16[3,1024,256]{2,0,1:T(4,128)(2,1)S(1)}, u32[]{:S(2)}, u32[]{:S(2)}) async-start(bf16[3,1024,256]{2,0,1:T(4,128)(2,1)} %copy.208), calls=%async_computation | async-start | bytes 4194304 | tf_op jit(solution)/shard_map/all_to_all | solution.py:114
  23.3 45.9 %all-to-all-done = bf16[3,1024,256]{2,0,1:T(4,128)(2,1)S(1)} async-done(((bf16[3,1024,256]{2,0,1:T(4,128)(2,1)}), bf16[3,1024,256]{2,0,1:T(4,128)(2,1)S(1)}, u32[]{:S(2)}, u32[]{:S(2)}) %all-to-all-start) | async-done | bytes 1572896 | tf_op jit(solution)/shard_map/all_to_all | solution.py:114
  84.2 4.4 %fusion.7 = (f32[256,16,128]{2,1,0:T(8,128)S(1)}, f32[256,16,128]{2,1,0:T(8,128)S(1)}, f32[256,16,128]{2,1,0:T(8,128)S(1)}, f32[256,16,128]{2,1,0:T(8,128)S(1)},...) fusion(f32[256,128,16]{1,2,0:T(8,128)S(1)} %fusion.194, f32[16,128]{1,0:T(8,128)S(1)} %get-tuple-element.42, ...), kind=kOutput, calls=%fused_computation.20 | convolution fusion | flops 59768832 | bytes 23613440 | tf_op jit(solution)/shard_map/kn,cnm->ckm/dot_general | solution.py:60
  88.7 2.5 %fusion.51 = f32[256,16,128]{2,0,1:T(8,128)S(1)} fusion(f32[256,16,128]{2,1,0:T(8,128)S(1)} %get-tuple-element.7), kind=kOutput, calls=%fused_computation.74 | convolution fusion | flops 805535744 | bytes 4194304 | tf_op jit(solution)/shard_map/ckn,nm->ckm/dot_general | solution.py:66
  91.2 2.8 %fusion.53 = f32[256,16,128]{2,0,1:T(8,128)S(1)} fusion(f32[256,16,128]{2,1,0:T(8,128)S(1)} %get-tuple-element.7), kind=kOutput, calls=%fused_computation.76 | convolution fusion | flops 805535744 | bytes 4194304 | tf_op jit(solution)/shard_map/ckn,nm->ckm/dot_general | solution.py:63
  94.0 2.5 %fusion.43 = f32[256,16,128]{2,0,1:T(8,128)S(1)} fusion(f32[256,16,128]{2,1,0:T(8,128)S(1)} %get-tuple-element.28), kind=kOutput, calls=%fused_computation.66 | convolution fusion | flops 805535744 | bytes 4194304 | tf_op jit(solution)/shard_map/ckn,nm->ckm/dot_general | solution.py:66
  96.5 2.6 %fusion.45 = f32[256,16,128]{2,0,1:T(8,128)S(1)} fusion(f32[256,16,128]{2,1,0:T(8,128)S(1)} %get-tuple-element.28), kind=kOutput, calls=%fused_computation.68 | convolution fusion | flops 805535744 | bytes 4194304 | tf_op jit(solution)/shard_map/ckn,nm->ckm/dot_general | solution.py:63
  99.1 2.5 %fusion.59 = f32[256,16,128]{2,0,1:T(8,128)S(1)} fusion(f32[256,16,128]{2,1,0:T(8,128)S(1)} %get-tuple-element.30), kind=kOutput, calls=%fused_computation.82 | convolution fusion | flops 805535744 | bytes 4194304 | tf_op jit(solution)/shard_map/ckn,nm->ckm/dot_general | solution.py:66
  101.6 3.0 %fusion.61 = f32[256,16,128]{2,0,1:T(8,128)S(1)} fusion(f32[256,16,128]{2,1,0:T(8,128)S(1)} %get-tuple-element.30), kind=kOutput, calls=%fused_computation.84 | convolution fusion | flops 805535744 | bytes 4194304 | tf_op jit(solution)/shard_map/ckn,nm->ckm/dot_general | solution.py:63
  104.6 2.6 %fusion.73 = f32[256,16,128]{2,0,1:T(8,128)S(1)} fusion(f32[256,16,128]{2,0,1:T(8,128)S(1)} %fusion.53, f32[256,16,128]{2,1,0:T(8,128)S(1)} %get-tuple-element.6), kind=kOutput, calls=%fused_computation.92 | convolution fusion | flops 806060032 | bytes 6291456 | tf_op jit(solution)/shard_map/ckn,nm->ckm/dot_general | solution.py:63
  107.2 2.6 %fusion.76 = f32[256,16,128]{2,0,1:T(8,128)S(1)} fusion(f32[256,16,128]{2,0,1:T(8,128)S(1)} %fusion.51, f32[256,16,128]{2,1,0:T(8,128)S(1)} %get-tuple-element.6), kind=kOutput, calls=%fused_computation.93 | convolution fusion | flops 806060032 | bytes 6291456 | tf_op jit(solution)/shard_map/ckn,nm->ckm/dot_general | solution.py:66
  109.8 2.6 %fusion.79 = f32[256,16,128]{2,0,1:T(8,128)S(1)} fusion(f32[256,16,128]{2,0,1:T(8,128)S(1)} %fusion.45, f32[256,16,128]{2,1,0:T(8,128)S(1)} %get-tuple-element.29), kind=kOutput, calls=%fused_computation.94 | convolution fusion | flops 806060032 | bytes 6291456 | tf_op jit(solution)/shard_map/ckn,nm->ckm/dot_general | solution.py:63
  112.4 2.6 %fusion.82 = f32[256,16,128]{2,0,1:T(8,128)S(1)} fusion(f32[256,16,128]{2,0,1:T(8,128)S(1)} %fusion.43, f32[256,16,128]{2,1,0:T(8,128)S(1)} %get-tuple-element.29), kind=kOutput, calls=%fused_computation.95 | convolution fusion | flops 806060032 | bytes 6291456 | tf_op jit(solution)/shard_map/ckn,nm->ckm/dot_general | solution.py:66
  115.1 2.7 %fusion.67 = f32[256,16,128]{2,0,1:T(8,128)S(1)} fusion(f32[256,16,128]{2,0,1:T(8,128)S(1)} %fusion.61, f32[256,16,128]{2,1,0:T(8,128)S(1)} %get-tuple-element.31), kind=kOutput, calls=%fused_computation.90 | convolution fusion | flops 806060032 | bytes 6291456 | tf_op jit(solution)/shard_map/ckn,nm->ckm/dot_general | solution.py:63
  117.8 3.5 %multiply_subtract_fusion.1 = (f32[256,16,128]{2,0,1:T(8,128)S(1)}, f32[256,16,128]{2,0,1:T(8,128)S(1)}, f32[256,16,128]{2,0,1:T(8,128)S(1)}, f32[256,16,128]{2,0,1:T(8,128)S(1)}) fusion(f32[256,16,128]{2,0,1:T(8,128)S(1)} %fusion.76, f32[256,16,128]{2,0,1:T(8,128)S(1)} %fusion.67, f32[256,16,128]{2,0,1:T(8,128)S(1)} %fusion.73, ...), kind=kOutput, calls=%fused_computation.49 | convolution fusion | flops 812351488 | bytes 23068672 | tf_op jit(solution)/shard_map/ckn,nm->ckm/dot_general | solution.py:66
  121.4 3.2 %fusion.35 = f32[256,16,128]{2,1,0:T(8,128)S(1)} fusion(f32[256,16,128]{2,0,1:T(8,128)S(1)} %get-tuple-element.3), kind=kOutput, calls=%fused_computation.58 | convolution fusion | flops 805535744 | bytes 4194304 | tf_op jit(solution)/shard_map/ckn,nm->ckm/dot_general | solution.py:79
  124.5 3.2 %fusion.37 = f32[256,16,128]{2,1,0:T(8,128)S(1)} fusion(f32[256,16,128]{2,0,1:T(8,128)S(1)} %get-tuple-element.3), kind=kOutput, calls=%fused_computation.60 | convolution fusion | flops 805535744 | bytes 4194304 | tf_op jit(solution)/shard_map/ckn,nm->ckm/dot_general | solution.py:76
  127.7 4.6 %fusion.27 = f32[256,16,128]{2,1,0:T(8,128)} fusion(f32[256,16,128]{2,0,1:T(8,128)S(1)} %get-tuple-element.12), kind=kOutput, calls=%fused_computation.50 | convolution fusion | flops 805535744 | bytes 4194304 | tf_op jit(solution)/shard_map/ckn,nm->ckm/dot_general | solution.py:79
  132.3 4.4 %fusion.29 = f32[256,16,128]{2,1,0:T(8,128)} fusion(f32[256,16,128]{2,0,1:T(8,128)S(1)} %get-tuple-element.12), kind=kOutput, calls=%fused_computation.52 | convolution fusion | flops 805535744 | bytes 4194304 | tf_op jit(solution)/shard_map/ckn,nm->ckm/dot_general | solution.py:76
  139.1 3.2 %fusion.88 = f32[256,16,128]{2,1,0:T(8,128)S(1)} fusion(f32[256,16,128]{2,1,0:T(8,128)S(1)} %fusion.35, f32[256,16,128]{2,0,1:T(8,128)S(1)} %get-tuple-element.2), kind=kOutput, calls=%fused_computation.97 | convolution fusion | flops 806060032 | bytes 6291456 | tf_op jit(solution)/shard_map/ckn,nm->ckm/dot_general | solution.py:79
  142.3 3.6 %fusion.85 = f32[256,16,128]{2,1,0:T(8,128)S(1)} fusion(f32[256,16,128]{2,1,0:T(8,128)S(1)} %fusion.37, f32[256,16,128]{2,0,1:T(8,128)S(1)} %get-tuple-element.2), kind=kOutput, calls=%fused_computation.96 | convolution fusion | flops 806060032 | bytes 6291456 | tf_op jit(solution)/shard_map/ckn,nm->ckm/dot_general | solution.py:76
  152.3 5.0 %fusion.94 = f32[256,16,128]{2,1,0:T(8,128)S(1)} fusion(f32[256,16,128]{2,1,0:T(8,128)} %fusion.27, f32[256,16,128]{2,0,1:T(8,128)S(1)} %get-tuple-element.13), kind=kOutput, calls=%fused_computation.99 | convolution fusion | flops 806060032 | bytes 6291456 | tf_op jit(solution)/shard_map/ckn,nm->ckm/dot_general | solution.py:79
  157.2 3.2 %fusion.91 = f32[256,16,128]{2,1,0:T(8,128)S(1)} fusion(f32[256,16,128]{2,1,0:T(8,128)S(1)} %copy-done.2, f32[256,16,128]{2,0,1:T(8,128)S(1)} %get-tuple-element.13), kind=kOutput, calls=%fused_computation.98 | convolution fusion | flops 806060032 | bytes 6291456 | tf_op jit(solution)/shard_map/ckn,nm->ckm/dot_general | solution.py:76
  161.9 2.6 %fusion.107 = f32[256,8,128]{2,1,0:T(8,128)} fusion(f32[256,128,8]{1,2,0:T(8,128)S(1)} %fusion.11, f32[256,16,128]{2,1,0:T(8,128)S(1)} %fusion.94, f32[256,16,128]{2,1,0:T(8,128)S(1)} %fusion.91, f32[16,128]{1,0:T(8,128)S(1)} %get-tuple-element.42, f32[16,128]{1,0:T(8,128)S(1)} %get-tuple-element.43, f32[16,16]{0,1:T(8,128)S(1)} %fusion.192), kind=kOutput, calls=%fused_computation.106 | convolution fusion | flops 52428800 | bytes 6308864 | tf_op jit(solution)/shard_map/nk,ckm->cnm/dot_general | solution.py:84
  164.5 2.5 %mul.900 = f32[1,256,1024]{2,1,0:T(8,128)} reshape(f32[256,8,128]{2,1,0:T(8,128)} %fusion.107) | data formatting | bytes 2097152 | tf_op jit(solution)/shard_map/mul | solution.py:87
  170.7 3.5 %all-to-all-start.1 = ((bf16[2,256,1024]{1,0,2:T(2,128)(2,1)}), bf16[2,256,1024]{1,0,2:T(2,128)(2,1)S(1)}, u32[]{:S(2)}, u32[]{:S(2)}) async-start(bf16[2,256,1024]{1,0,2:T(2,128)(2,1)} %copy.245), calls=%async_computation.1 | async-start | bytes 2097152 | tf_op jit(solution)/shard_map/all_to_all | solution.py:118
  174.3 25.2 %all-to-all-done.1 = bf16[2,256,1024]{1,0,2:T(2,128)(2,1)S(1)} async-done(((bf16[2,256,1024]{1,0,2:T(2,128)(2,1)}), bf16[2,256,1024]{1,0,2:T(2,128)(2,1)S(1)}, u32[]{:S(2)}, u32[]{:S(2)}) %all-to-all-start.1) | async-done | bytes 1048608 | tf_op jit(solution)/shard_map/all_to_all | solution.py:118
  207.8 4.4 %collective-permute-done.1 = f32[3,1024,2]{1,0,2:T(4,128)S(1)} collective-permute-done((f32[3,1024,2]{1,0,2:T(4,128)S(1)}, f32[3,1024,2]{1,0,2:T(4,128)S(1)}, u32[]{:S(2)}, u32[]{:S(2)}) %collective-permute-start.1) | collective-permute-done | bytes 24608 | tf_op jit(solution)/shard_map/ppermute | solution.py:13
  215.6 3.9 %fusion.2 = bf16[3,1024,256]{2,1,0:T(8,128)(2,1)} fusion(f32[3,1024,258]{2,1,0:T(8,128)S(1)} %pad_maximum_fusion, f32[256]{0:T(256)S(1)} %get-tuple-element.33, f32[256]{0:T(256)S(1)} %get-tuple-element.34, f32[256]{0:T(256)S(1)} %get-tuple-element.32, f32[3,1024]{1,0:T(4,128)S(1)} %get-tuple-element.40, f32[3,1024]{1,0:T(4,128)S(1)} %get-tuple-element.41, ...), kind=kLoop, calls=%fused_computation.4 | loop fusion | flops 8650752 | bytes 11049984 | tf_op jit(solution)/shard_map/convert_element_type | solution.py:153
  (86 shorter events, 46.5 us)
Async XLA Ops:
  0.6 8.6 %copy-start.8 = (bf16[3,1024,256]{2,1,0:T(8,128)(2,1)S(1)}, bf16[3,1024,256]{2,1,0:T(8,128)(2,1)}, u32[]{:S(2)}) copy-start(bf16[3,1024,256]{2,1,0:T(8,128)(2,1)} %param.6) | copy-start | bytes 4718596
  0.6 6.8 %copy-start.14 = (s32[16]{0:T(128)S(1)}, s32[16]{0:T(128)}, u32[]{:S(2)}) copy-start(s32[16]{0:T(128)} %param.11) | copy-start | bytes 196
  0.6 7.1 %copy-start.13 = (f32[3,3,1024]{2,1,0:T(4,128)S(1)}, f32[3,3,1024]{2,1,0:T(4,128)}, u32[]{:S(2)}) copy-start(f32[3,3,1024]{2,1,0:T(4,128)} %param.9) | copy-start | bytes 110596
  2.5 6.3 %collective-permute-start = (bf16[3,1024,2]{1,2,0:T(2,128)(2,1)S(1)}, bf16[3,1024,2]{1,2,0:T(2,128)(2,1)S(1)}, u32[]{:S(2)}, u32[]{:S(2)}) collective-permute-start(bf16[3,1024,2]{1,2,0:T(2,128)(2,1)S(1)} %copy.272), channel_id=1, source_target_pairs={{0,4},{4,8},{8,12},{1,5},{5,9},{9,13},{2,6},{6,10},{10,14},{3,7},{... | collective-permute-start | bytes 36872 | tf_op jit(solution)/shard_map/ppermute | solution.py:13
  9.3 4.2 %copy-start.10 = (bf16[1024,256]{1,0:T(8,128)(2,1)S(1)}, bf16[1024,256]{1,0:T(8,128)(2,1)}, u32[]{:S(2)}) copy-start(bf16[1024,256]{1,0:T(8,128)(2,1)} %param.7) | copy-start | bytes 1572868
  12.3 1.1 copy-start
  12.3 1.4 copy-start.12
  16.6 52.6 %all-to-all-start = ((bf16[3,1024,256]{2,0,1:T(4,128)(2,1)}), bf16[3,1024,256]{2,0,1:T(4,128)(2,1)S(1)}, u32[]{:S(2)}, u32[]{:S(2)}) async-start(bf16[3,1024,256]{2,0,1:T(4,128)(2,1)} %copy.208), calls=%async_computation | async-start | bytes 4194304 | tf_op jit(solution)/shard_map/all_to_all | solution.py:114
  75.6 4.7 %copy-start.9 = (bf16[1,256,4,256]{3,1,2,0:T(8,128)(2,1)S(1)}, bf16[1,256,4,256]{3,1,2,0:T(8,128)(2,1)}, u32[]{:S(2)}) copy-start(bf16[1,256,4,256]{3,1,2,0:T(8,128)(2,1)} %get-tuple-element.19) | copy-start | bytes 1572868
  82.6 1.6 copy-start.3
  132.3 4.4 %copy-start.5 = (f32[1,4,32,8,256]{4,3,2,1,0:T(8,128)S(1)}, f32[1,4,32,8,256]{4,3,2,1,0:T(8,128)}, u32[]{:S(2)}) copy-start(f32[1,4,32,8,256]{4,3,2,1,0:T(8,128)} %get-tuple-element.16) | copy-start | bytes 3145732
  136.8 1.2 copy-start.4
  152.3 5.0 %copy-start.2 = (f32[256,16,128]{2,1,0:T(8,128)S(1)}, f32[256,16,128]{2,1,0:T(8,128)}, u32[]{:S(2)}) copy-start(f32[256,16,128]{2,1,0:T(8,128)} %fusion.29) | copy-start | bytes 6291460
  164.5 2.5 %copy-start.6 = (f32[1,4,32,8,256]{4,3,1,2,0:T(8,128)S(1)}, f32[1,4,32,8,256]{4,3,1,2,0:T(8,128)}, u32[]{:S(2)}) copy-start(f32[1,4,32,8,256]{4,3,1,2,0:T(8,128)} %copy.274) | copy-start | bytes 3145732
  164.5 2.5 %copy-start.7 = (f32[1,256,1024]{2,1,0:T(8,128)S(1)}, f32[1,256,1024]{2,1,0:T(8,128)}, u32[]{:S(2)}) copy-start(f32[1,256,1024]{2,1,0:T(8,128)} %mul.883) | copy-start | bytes 3145732
  170.7 28.8 %all-to-all-start.1 = ((bf16[2,256,1024]{1,0,2:T(2,128)(2,1)}), bf16[2,256,1024]{1,0,2:T(2,128)(2,1)S(1)}, u32[]{:S(2)}, u32[]{:S(2)}) async-start(bf16[2,256,1024]{1,0,2:T(2,128)(2,1)} %copy.245), calls=%async_computation.1 | async-start | bytes 2097152 | tf_op jit(solution)/shard_map/all_to_all | solution.py:118
  200.2 1.4 copy-start.1
  200.3 1.6 copy-start.11
  206.4 5.8 %collective-permute-start.1 = (f32[3,1024,2]{1,0,2:T(4,128)S(1)}, f32[3,1024,2]{1,0,2:T(4,128)S(1)}, u32[]{:S(2)}, u32[]{:S(2)}) collective-permute-start(f32[3,1024,2]{1,0,2:T(4,128)S(1)} %copy.247), channel_id=1, source_target_pairs={{4,0},{8,4},{12,8},{5,1},{9,5},{13,9},{6,2},{10,6},{14,10},{7,3},{... | collective-permute-start | bytes 73736 | tf_op jit(solution)/shard_map/ppermute | solution.py:13
where the time goes:
time: 224 us; the launch traced here: 220 us
  matrix products  84.5 us (38%)
  waiting for transfers between devices  76.5 us (34%)
  local copies, waits for them, and re-layouts  27.4 us (12%)
  starting transfers between devices  15.5 us (7%)
  other arithmetic  14.5 us (6%)
    all_to_all x1, waiting for transfers between devices, to_channels(): lax.all_to_all(stacked, 'seq', split_axis=1, concat_axis=2, tiled=True)  45.9 us
    all_to_all x1, waiting for transfers between devices, to_sequence(): lax.all_to_all(stacked, 'seq', split_axis=2, concat_axis=1, tiled=True)  25.2 us
    dot_general x3, matrix products, forward_transform(): jnp.einsum('ckn,nm->ckm', turned_re, col_im, precision=HIGHEST)  8.84 us
    dot_general x3, matrix products, forward_transform(): jnp.einsum('ckn,nm->ckm', turned_im, col_im, precision=HIGHEST)  8.28 us
    dot_general x2, matrix products, inverse_transform(): jnp.einsum('ckn,nm->ckm', spec_re, col_im, precision=HIGHEST)  8.19 us
    dot_general x3, matrix products, forward_transform(): jnp.einsum('ckn,nm->ckm', turned_re, col_re, precision=HIGHEST)  7.87 us
    dot_general x3, matrix products, forward_transform(): jnp.einsum('kn,cnm->ckm', row_im[:, :half_rows], blocks_in, precision=HIG...  7.82 us
    dot_general x2, matrix products, inverse_transform(): jnp.einsum('ckn,nm->ckm', spec_im, col_re, precision=HIGHEST)  7.78 us
  transfers between devices with their start and end apart: 4, of which 4 were waited for; matrix products, arithmetic and copies ran while one was open for 1% of the time, Pallas kernels for 0%

commit v1 on v0

--- a/solution.py
+++ b/solution.py
@@ -1,4 +1,5 @@
 import jax
+import numpy as np
 import jax.numpy as jnp
 from jax import lax
 from jax.sharding import PartitionSpec as P
@@ -107,6 +108,46 @@
     )
     y_out = (conv_out + skip_part[:, None] * mixed_f).astype(jnp.bfloat16)
     dmixed = (corr_out + skip_part[:, None] * grad_f).astype(jnp.bfloat16)
+    return (y_out, dmixed)
+
+
+DENSE_MAX = 1024
+FINE = 32
+
+
+def angle_parts(length):
+    base = np.arange(length, dtype=np.int64) * 4 + 1
+    fine = np.arange(FINE, dtype=np.int64)[:, None] * base[None, :] % (4 * length)
+    coarse = np.arange(0, length, FINE, dtype=np.int64)[:, None] * base[None, :] % (4 * length)
+    scale = 2.0 * np.pi / (4 * length)
+    return [
+        func(part * scale).astype(np.float32)
+        for part in (coarse, fine)
+        for func in (np.cos, np.sin)
+    ]
+
+
+def dense_filter(filt, mixed_in, grad_in, skip_part):
+    length = mixed_in.shape[1]
+    cc, cs, fc, fs = [jnp.asarray(p)[:, None] if i < 2 else jnp.asarray(p)[None] for i, p in enumerate(angle_parts(length))]
+    cos_t = (cc * fc - cs * fs).reshape(length, length)
+    sin_t = (cs * fc + cc * fs).reshape(length, length)
+    table = jnp.concatenate([cos_t, sin_t], axis=1).astype(jnp.bfloat16)
+
+    def fwd(x):
+        return jnp.dot(x, table, preferred_element_type=jnp.float32)
+
+    def inv(x):
+        return lax.dot_general(x.astype(jnp.bfloat16), table, (((1,), (1,)), ((), ())), preferred_element_type=jnp.float32) * (1.0 / length)
+
+    h, m, g = fwd(filt), fwd(mixed_in), fwd(grad_in)
+    hc, hs = h[:, :length], h[:, length:]
+    mc, ms = m[:, :length], m[:, length:]
+    gc, gs = g[:, :length], g[:, length:]
+    conv_out = inv(jnp.concatenate([hc * mc - hs * ms, hc * ms + hs * mc], axis=1))
+    corr_out = inv(jnp.concatenate([hc * gc + hs * gs, hc * gs - hs * gc], axis=1))
+    y_out = (conv_out + skip_part[:, None] * mixed_in.astype(jnp.float32)).astype(jnp.bfloat16)
+    dmixed = (corr_out + skip_part[:, None] * grad_in.astype(jnp.float32)).astype(jnp.bfloat16)
     return (y_out, dmixed)
 
 
@@ -139,7 +180,8 @@
     grad_in = (dout_f * query_side).astype(jnp.bfloat16)
     moved = to_channels(jnp.stack([mixed, grad_in, filters]))
     skip_part = lax.dynamic_slice_in_dim(skip, seq_rank * chan_part, chan_part, 0)
-    y_out, dmixed = long_filter(moved[2], moved[0], moved[1], skip_part)
+    run = dense_filter if moved.shape[2] <= DENSE_MAX else long_filter
+    y_out, dmixed = run(moved[2], moved[0], moved[1], skip_part)
     returned = to_sequence(jnp.stack([y_out, dmixed]))
     y_here = returned[0].astype(jnp.float32)
     dmixed_here = returned[1].astype(jnp.float32)

time: 224 us -> 134 us (0.60); the launches traced: 220 us -> 133 us
  matrix products: 84.5 us -> 6.44 us
  local copies, waits for them, and re-layouts: 27.4 us -> 20 us
  other arithmetic: 14.5 us -> 18.5 us
  waiting for transfers between devices: 76.5 us -> 73.1 us
    dot_general x30 -> x5, matrix products: 84.5 us -> 6.44 us  [the longest x3 3.81 us: fwd(): return jnp.dot(x, table, preferred_element_type=jnp.float32)]
    mul x2 -> x0, local copies, waits for them, and re-layouts: 4.89 us -> none  [inverse_transform(): signal.reshape(signal.shape[0], half_rows * 128) * (1.0 / (rows_n * 128))]
    another operation x2 -> x4, other arithmetic: 0.16 us -> 4.55 us
    all_to_all x1, waiting for transfers between devices: 45.9 us -> 43.4 us  [to_channels(): lax.all_to_all(stacked, 'seq', split_axis=1, concat_axis=2, tiled=True)]
  transfers between devices with their start and end apart: 4 -> 4, of which waited for: 4 -> 3; matrix products, arithmetic and copies ran while one was open for 1% -> 5% of each run, Pallas kernels for 0% -> 0%
where the time goes in v1:
time: 134 us; the launch traced here: 133 us
  waiting for transfers between devices  73.1 us (55%)
  local copies, waits for them, and re-layouts  20 us (15%)
  other arithmetic  18.5 us (14%)
  starting transfers between devices  14.1 us (11%)
  matrix products  6.44 us (5%)
    all_to_all x1, waiting for transfers between devices, to_channels(): lax.all_to_all(stacked, 'seq', split_axis=1, concat_axis=2, tiled=True)  43.4 us
    all_to_all x1, waiting for transfers between devices, to_sequence(): lax.all_to_all(stacked, 'seq', split_axis=2, concat_axis=1, tiled=True)  25.3 us
    ppermute x2, starting transfers between devices, shifted(): lax.ppermute(value, axis, [(source, source + steps) for source in range(l...  6.25 us
    another operation x4, other arithmetic  4.55 us
    ppermute x2, waiting for transfers between devices, shifted(): lax.ppermute(value, axis, [(source, source + steps) for source in range(l...  4.44 us
    all_to_all x1, starting transfers between devices, to_channels(): lax.all_to_all(stacked, 'seq', split_axis=1, concat_axis=2, tiled=True)  4.31 us
    convert_element_type x1, other arithmetic, local(): short_backward(grads_ext, taps, offsets_ext).astype(jnp.bfloat16)  3.92 us
    dot_general x3, matrix products, fwd(): return jnp.dot(x, table, preferred_element_type=jnp.float32)  3.81 us
  transfers between devices with their start and end apart: 4, of which 3 were waited for; matrix products, arithmetic and copies ran while one was open for 5% of the time, Pallas kernels for 0%

profile of v1, /device:TPU:0, one launch (start us, length us, event | category | flops | bytes accessed | tf_op | source)
XLA Modules:
  0.0 133.1 jit_solution(16036028812956328695)
XLA Ops:
  0.6 1.5 %slice.88 = bf16[3,1024,2]{2,1,0:T(8,128)(2,1)S(1)} slice(bf16[3,1024,256]{2,1,0:T(8,128)(2,1)} %param.10), slice={[0:3], [0:1024], [254:256]} | slice | bytes 24576 | tf_op jit(solution)/shard_map/slice | solution.py:170
  2.5 5.0 %collective-permute-start = (bf16[3,1024,2]{1,2,0:T(2,128)(2,1)S(1)}, bf16[3,1024,2]{1,2,0:T(2,128)(2,1)S(1)}, u32[]{:S(2)}, u32[]{:S(2)}) collective-permute-start(bf16[3,1024,2]{1,2,0:T(2,128)(2,1)S(1)} %copy.50), channel_id=1, source_target_pairs={{0,4},{4,8},{8,12},{1,5},{5,9},{9,13},{2,6},{6,10},{10,14},{3,7},{... | collective-permute-start | bytes 36872 | tf_op jit(solution)/shard_map/ppermute | solution.py:14
  8.3 0.9 fusion.32
  9.3 0.7 select_reduce_fusion.1
  10.5 3.0 %add_convert_fusion.1 = bf16[3,1024,256]{2,1,0:T(8,128)(2,1)S(1)} fusion(bf16[3,1024,256]{2,1,0:T(8,128)(2,1)S(1)} %copy-done.1, bf16[3,1024,2]{2,1,0:T(8,128)(2,1)S(1)} %copy.40, f32[256]{0:T(256)S(1)} %get-tuple-element.27, f32[3,1024]{1,0:T(4,128)S(1)} %get-tuple-element.28, f32[256]{0:T(256)S(1)} %get-tuple-element.26, ...), kind=kLoop, calls=%fused_computation.12 | loop fusion | flops 14155776 | bytes 3197952 | tf_op jit(solution)/shard_map/convert_element_type | solution.py:174
  13.7 1.0 copy-done
  15.1 2.7 %copy.41 = bf16[3,1024,256]{2,0,1:T(4,128)(2,1)} copy(bf16[3,1024,256]{2,1,0:T(8,128)(2,1)S(1)} %pad_maximum_fusion.4) | data formatting | bytes 3145728 | tf_op jit(solution)/shard_map/stack | solution.py:181
  17.8 4.3 %all-to-all-start = ((bf16[3,1024,256]{2,0,1:T(4,128)(2,1)}), bf16[3,1024,256]{2,0,1:T(4,128)(2,1)S(1)}, u32[]{:S(2)}, u32[]{:S(2)}) async-start(bf16[3,1024,256]{2,0,1:T(4,128)(2,1)} %copy.41), calls=%async_computation | async-start | bytes 4194304 | tf_op jit(solution)/shard_map/all_to_all | solution.py:155
  22.1 0.8 dynamic_slice.3
  22.9 3.4 %subtract_convert_fusion = (bf16[32,32,1024]{2,1,0:T(8,128)(2,1)}, bf16[32,32,1024]{2,1,0:T(8,128)(2,1)}) fusion(f32[32,1024]{1,0:T(8,128)S(1)} %copy-done.10, f32[32,1024]{1,0:T(8,128)S(1)} %copy-done.8, f32[32,1024]{1,0:T(8,128)S(1)} %copy-done.9, f32[32,1024]{1,0:T(8,128)S(1)} %copy-done.7), kind=kLoop, calls=%fused_computation.3 | loop fusion | flops 8388608 | bytes 4718592 | tf_op jit(solution)/shard_map/convert.10
  26.3 43.4 %all-to-all-done = bf16[3,1024,256]{2,0,1:T(4,128)(2,1)S(1)} async-done(((bf16[3,1024,256]{2,0,1:T(4,128)(2,1)}), bf16[3,1024,256]{2,0,1:T(4,128)(2,1)S(1)}, u32[]{:S(2)}, u32[]{:S(2)}) %all-to-all-start) | async-done | bytes 1572896 | tf_op jit(solution)/shard_map/all_to_all | solution.py:155
  69.7 1.5 %copy.58 = bf16[3,4,256,256]{3,1,2,0:T(4,128)(2,1)S(1)} copy(bf16[3,4,256,256]{3,0,2,1:T(4,128)(2,1)S(1)} %bitcast.52) | data formatting | bytes 3145728 | tf_op jit(solution)/shard_map/all_to_all | solution.py:155
  72.0 0.8 copy-done.2
  73.4 1.3 fusion.27
  74.7 1.3 fusion.29
  76.1 1.3 fusion.28
  77.4 1.0 subtract_convert_fusion.2
  78.3 1.3 fusion.10
  79.7 1.3 fusion.11
  81.1 2.0 %copy.43 = bf16[2,256,1024]{1,0,2:T(2,128)(2,1)} copy(bf16[2,256,1024]{2,1,0:T(8,128)(2,1)S(1)} %pad_maximum_fusion.5) | data formatting | bytes 2097152 | tf_op jit(solution)/shard_map/stack | solution.py:185
  83.1 3.5 %all-to-all-start.1 = ((bf16[2,256,1024]{1,0,2:T(2,128)(2,1)}), bf16[2,256,1024]{1,0,2:T(2,128)(2,1)S(1)}, u32[]{:S(2)}, u32[]{:S(2)}) async-start(bf16[2,256,1024]{1,0,2:T(2,128)(2,1)} %copy.43), calls=%async_computation.1 | async-start | bytes 2097152 | tf_op jit(solution)/shard_map/all_to_all | solution.py:159
  86.8 25.3 %all-to-all-done.1 = bf16[2,256,1024]{1,0,2:T(2,128)(2,1)S(1)} async-done(((bf16[2,256,1024]{1,0,2:T(2,128)(2,1)}), bf16[2,256,1024]{1,0,2:T(2,128)(2,1)S(1)}, u32[]{:S(2)}, u32[]{:S(2)}) %all-to-all-start.1) | async-done | bytes 1048608 | tf_op jit(solution)/shard_map/all_to_all | solution.py:159
  112.0 0.7 copy.44
  112.9 1.5 %convert_multiply_fusion.1 = (f32[1,1024,256]{2,1,0:T(8,128)S(1)}, f32[1,1024,256]{2,1,0:T(8,128)S(1)}) fusion(bf16[1,4,256,256]{3,2,1,0:T(8,128)(2,1)S(1)} %get-tuple-element.13, bf16[3,1024,256]{2,1,0:T(8,128)(2,1)} %copy-done), kind=kLoop, calls=%fused_computation.22 | loop fusion | flops 1310720 | bytes 3670016 | tf_op jit(solution)/shard_map/mul | solution.py:189
  114.4 2.1 %fusion.15 = (f32[1,1024,256]{2,1,0:T(8,128)S(1)}, bf16[1024,256]{1,0:T(8,128)(2,1)}) fusion(bf16[1024,256]{1,0:T(8,128)(2,1)S(1)} %copy-done.5, bf16[1,4,256,256]{3,2,1,0:T(8,128)(2,1)S(1)} %get-tuple-element.14, bf16[3,1024,256]{2,1,0:T(8,128)(2,1)} %copy-done), kind=kLoop, calls=%fused_computation.36 | loop fusion | flops 1572864 | bytes 3145728 | tf_op jit(solution)/shard_map/stack | solution.py:189
  116.7 1.2 slice.128
  117.9 2.0 %copy.45 = f32[3,1024,2]{1,0,2:T(4,128)S(1)} copy(f32[3,1024,2]{2,1,0:T(8,128)} %slice.128) | data formatting | bytes 49152 | tf_op jit(solution)/shard_map/slice | solution.py:190
  119.9 1.3 collective-permute-start.1
  121.3 4.4 %collective-permute-done.1 = f32[3,1024,2]{1,0,2:T(4,128)S(1)} collective-permute-done((f32[3,1024,2]{1,0,2:T(4,128)S(1)}, f32[3,1024,2]{1,0,2:T(4,128)S(1)}, u32[]{:S(2)}, u32[]{:S(2)}) %collective-permute-start.1) | collective-permute-done | bytes 24608 | tf_op jit(solution)/shard_map/ppermute | solution.py:14
  125.7 1.6 %copy.46 = f32[3,1024,2]{2,1,0:T(8,128)} copy(f32[3,1024,2]{1,0,2:T(4,128)S(1)} %collective-permute-done.1) | data formatting | bytes 49152 | tf_op jit(solution)/shard_map/ppermute | solution.py:14
  127.4 1.7 %pad_maximum_fusion = f32[3,1024,258]{2,1,0:T(8,128)S(1)} fusion(f32[3,1024,2]{2,1,0:T(8,128)} %copy.46, f32[1,1024,256]{2,1,0:T(8,128)S(1)} %get-tuple-element.7, f32[1,1024,256]{2,1,0:T(8,128)S(1)} %get-tuple-element.6, f32[1,1024,256]{2,1,0:T(8,128)S(1)} %get-tuple-element.15), kind=kLoop, calls=%fused_computation | loop fusion | flops 2377728 | bytes 6340608 | tf_op jit(solution)/shard_map/concatenate | solution.py:191
  129.1 3.9 %fusion.2 = bf16[3,1024,256]{2,1,0:T(8,128)(2,1)} fusion(f32[3,1024,258]{2,1,0:T(8,128)S(1)} %pad_maximum_fusion, f32[256]{0:T(256)S(1)} %get-tuple-element.23, f32[256]{0:T(256)S(1)} %get-tuple-element.24, f32[256]{0:T(256)S(1)} %get-tuple-element.22, f32[3,1024]{1,0:T(4,128)S(1)} %get-tuple-element.28, f32[3,1024]{1,0:T(4,128)S(1)} %get-tuple-element.29, ...), kind=kLoop, calls=%fused_computation.7 | loop fusion | flops 8650752 | bytes 11049984 | tf_op jit(solution)/shard_map/convert_element_type | solution.py:195
  (46 shorter events, 4.2 us)
Async XLA Ops:
  0.6 9.9 %copy-start.1 = (bf16[3,1024,256]{2,1,0:T(8,128)(2,1)S(1)}, bf16[3,1024,256]{2,1,0:T(8,128)(2,1)}, u32[]{:S(2)}) copy-start(bf16[3,1024,256]{2,1,0:T(8,128)(2,1)} %param.10) | copy-start | bytes 4718596
  2.5 7.6 %collective-permute-start = (bf16[3,1024,2]{1,2,0:T(2,128)(2,1)S(1)}, bf16[3,1024,2]{1,2,0:T(2,128)(2,1)S(1)}, u32[]{:S(2)}, u32[]{:S(2)}) collective-permute-start(bf16[3,1024,2]{1,2,0:T(2,128)(2,1)S(1)} %copy.50), channel_id=1, source_target_pairs={{0,4},{4,8},{8,12},{1,5},{5,9},{9,13},{2,6},{6,10},{10,14},{3,7},{... | collective-permute-start | bytes 36872 | tf_op jit(solution)/shard_map/ppermute | solution.py:14
  10.1 4.6 %copy-start.4 = (bf16[1024,256]{1,0:T(8,128)(2,1)S(1)}, bf16[1024,256]{1,0:T(8,128)(2,1)}, u32[]{:S(2)}) copy-start(bf16[1024,256]{1,0:T(8,128)(2,1)} %param.11) | copy-start | bytes 1572868
  10.5 4.3 %copy-start.6 = (bf16[1024,256]{1,0:T(8,128)(2,1)S(1)}, bf16[1024,256]{1,0:T(8,128)(2,1)}, u32[]{:S(2)}) copy-start(bf16[1024,256]{1,0:T(8,128)(2,1)} %param.12) | copy-start | bytes 1572868
  13.6 1.1 copy-start
  15.1 7.8 %copy-start.7 = (f32[32,1024]{1,0:T(8,128)S(1)}, f32[32,1024]{1,0:T(8,128)}, u32[]{:S(2)}) copy-start(f32[32,1024]{1,0:T(8,128)} %constant.32.clone) | copy-start | bytes 393220
  15.1 7.8 %copy-start.8 = (f32[32,1024]{1,0:T(8,128)S(1)}, f32[32,1024]{1,0:T(8,128)}, u32[]{:S(2)}) copy-start(f32[32,1024]{1,0:T(8,128)} %constant.33.clone) | copy-start | bytes 393220
  15.1 7.8 %copy-start.9 = (f32[32,1024]{1,0:T(8,128)S(1)}, f32[32,1024]{1,0:T(8,128)}, u32[]{:S(2)}) copy-start(f32[32,1024]{1,0:T(8,128)} %constant.34.clone) | copy-start | bytes 393220
  15.1 7.8 %copy-start.10 = (f32[32,1024]{1,0:T(8,128)S(1)}, f32[32,1024]{1,0:T(8,128)}, u32[]{:S(2)}) copy-start(f32[32,1024]{1,0:T(8,128)} %constant.35.clone) | copy-start | bytes 393220
  17.8 51.9 %all-to-all-start = ((bf16[3,1024,256]{2,0,1:T(4,128)(2,1)}), bf16[3,1024,256]{2,0,1:T(4,128)(2,1)S(1)}, u32[]{:S(2)}, u32[]{:S(2)}) async-start(bf16[3,1024,256]{2,0,1:T(4,128)(2,1)} %copy.41), calls=%async_computation | async-start | bytes 4194304 | tf_op jit(solution)/shard_map/all_to_all | solution.py:155
  71.2 1.6 %copy-start.2 = (bf16[32,32,1024]{2,1,0:T(8,128)(2,1)S(1)}, bf16[32,32,1024]{2,1,0:T(8,128)(2,1)}, u32[]{:S(2)}) copy-start(bf16[32,32,1024]{2,1,0:T(8,128)(2,1)} %get-tuple-element.17) | copy-start | bytes 6291460
  71.2 2.2 %copy-start.3 = (bf16[32,32,1024]{2,1,0:T(8,128)(2,1)S(1)}, bf16[32,32,1024]{2,1,0:T(8,128)(2,1)}, u32[]{:S(2)}) copy-start(bf16[32,32,1024]{2,1,0:T(8,128)(2,1)} %get-tuple-element.18) | copy-start | bytes 6291460
  81.0 5.7 %copy-start.11 = (s32[16]{0:T(128)S(1)}, s32[16]{0:T(128)}, u32[]{:S(2)}) copy-start(s32[16]{0:T(128)} %param.15) | copy-start | bytes 196
  83.1 28.9 %all-to-all-start.1 = ((bf16[2,256,1024]{1,0,2:T(2,128)(2,1)}), bf16[2,256,1024]{1,0,2:T(2,128)(2,1)S(1)}, u32[]{:S(2)}, u32[]{:S(2)}) async-start(bf16[2,256,1024]{1,0,2:T(2,128)(2,1)} %copy.43), calls=%async_computation.1 | async-start | bytes 2097152 | tf_op jit(solution)/shard_map/all_to_all | solution.py:159
  112.8 1.6 %copy-start.5 = (bf16[1024,256]{1,0:T(8,128)(2,1)S(1)}, bf16[1024,256]{1,0:T(8,128)(2,1)}, u32[]{:S(2)}) copy-start(bf16[1024,256]{1,0:T(8,128)(2,1)} %param.11) | copy-start | bytes 1572868
  119.9 5.8 %collective-permute-start.1 = (f32[3,1024,2]{1,0,2:T(4,128)S(1)}, f32[3,1024,2]{1,0,2:T(4,128)S(1)}, u32[]{:S(2)}, u32[]{:S(2)}) collective-permute-start(f32[3,1024,2]{1,0,2:T(4,128)S(1)} %copy.45), channel_id=1, source_target_pairs={{4,0},{8,4},{12,8},{5,1},{9,5},{13,9},{6,2},{10,6},{14,10},{7,3},{... | collective-permute-start | bytes 73736 | tf_op jit(solution)/shard_map/ppermute | solution.py:14

commit v2 on v1

--- a/solution.py
+++ b/solution.py
@@ -1,7 +1,11 @@
+import functools
+
 import jax
 import numpy as np
 import jax.numpy as jnp
 from jax import lax
+from jax.experimental import pallas as pl
+from jax.experimental.pallas import tpu as pltpu
 from jax.sharding import PartitionSpec as P
 
 HIGHEST = lax.Precision.HIGHEST
@@ -159,7 +163,7 @@
     return lax.all_to_all(stacked, "seq", split_axis=2, concat_axis=1, tiled=True)
 
 
-def local(features, dout, filters, taps, skip, lengths):
+def local_general(features, dout, filters, taps, skip, lengths):
     blocks = lax.axis_size("seq")
     seq_rank = lax.axis_index("seq")
     span_rows = features.shape[2]
@@ -196,6 +200,378 @@
     return (out, dfeatures)
 
 
+HALF = 128
+NN = (((1,), (0,)), ((), ()))
+NT = (((1,), (1,)), ((), ()))
+TN = (((0,), (0,)), ((), ()))
+
+
+def mm(a, b, dims=NN):
+    return lax.dot_general(a, b, dims, preferred_element_type=jnp.float32)
+
+
+def mixer_kernel(
+    n,
+    lengths_ref, feat_ref, dout_ref, filt_ref, par_ref, tab_ref,
+    out_ref, df_ref,
+    rim_src, rim, shift_m, place, keep_s, q_s, k_s, v_s, d_s,
+    fwd_send, fwd_recv, filt_recv, table, spec_h, spec, y_send, y_recv, hal_src, hal,
+    rim_ss, rim_rs, filt_ss, filt_rs, fwd_ss, fwd_rs, y_ss, y_rs, hal_ss, hal_rs,
+):
+    rank = lax.axis_index("seq")
+    span = feat_ref.shape[2]
+    part = feat_ref.shape[1] // n
+    subs = part // HALF
+    length = span * n
+    wide = span + 128
+    bf = jnp.bfloat16
+    f32 = jnp.float32
+
+    def peer(step):
+        return lax.rem(rank + 1 + step, n)
+
+    barrier = pltpu.get_barrier_semaphore()
+    for step in range(n - 1):
+        pl.semaphore_signal(barrier, inc=1, device_id={"seq": peer(step)}, device_id_type=pl.DeviceIdType.MESH)
+
+    def remote(src, dst, ss, rs, dest):
+        return pltpu.make_async_remote_copy(
+            src_ref=src, dst_ref=dst, send_sem=ss, recv_sem=rs,
+            device_id={"seq": dest}, device_id_type=pl.DeviceIdType.MESH,
+        )
+
+    def rim_copy(side, dest):
+        return remote(rim_src, rim.at[pl.ds(16 * side, 16)], rim_ss.at[side], rim_rs.at[side], dest)
+
+    def filt_copy(who, dest):
+        rows = pl.ds(pl.multiple_of(dest * part, HALF), part)
+        cols = pl.ds(pl.multiple_of(who * span, 128), span)
+        return remote(filt_ref.at[rows], filt_recv.at[:, cols], filt_ss.at[dest], filt_rs.at[who], dest)
+
+    def fwd_copy(sub, who, dest):
+        cols = pl.ds(pl.multiple_of(who * span, 128), span)
+        return remote(fwd_send.at[sub, dest], fwd_recv.at[sub, :, cols], fwd_ss.at[sub, dest], fwd_rs.at[sub, who], dest)
+
+    def y_copy(sub, who, dest):
+        return remote(y_send.at[sub, dest], y_recv.at[sub, who], y_ss.at[sub, dest], y_rs.at[sub, who], dest)
+
+    def hal_copy(sub, dest):
+        return remote(hal_src.at[sub], hal.at[sub], hal_ss.at[sub], hal_rs.at[sub], dest)
+
+    r_id = lax.broadcasted_iota(jnp.int32, (16, span), 0)
+    p_id = lax.broadcasted_iota(jnp.int32, (16, span), 1)
+    total = None
+    for a in range(4):
+        hit = (
+            ((r_id == 4 * a) & (p_id == span - 2)) | ((r_id == 4 * a + 1) & (p_id == span - 1))
+            | ((r_id == 4 * a + 2) & (p_id == 0)) | ((r_id == 4 * a + 3) & (p_id == 1))
+        )
+        pick = jnp.where(hit, 1.0, 0.0).astype(bf)
+        term = mm(pick, feat_ref[a] if a < 3 else dout_ref[...], NT)
+        total = term if total is None else total + term
+    rim_src[...] = total.astype(bf)
+
+    @pl.when(rank == 0)
+    def _():
+        rim[0:16, :] = jnp.zeros((16, rim.shape[1]), bf)
+
+    @pl.when(rank == n - 1)
+    def _():
+        rim[16:32, :] = jnp.zeros((16, rim.shape[1]), bf)
+        for sub in range(subs):
+            hal[sub] = jnp.zeros(hal.shape[1:], bf)
+
+    pl.semaphore_wait(barrier, n - 1)
+
+    @pl.when(rank < n - 1)
+    def _():
+        rim_copy(0, rank + 1).start()
+
+    @pl.when(rank > 0)
+    def _():
+        rim_copy(1, rank - 1).start()
+
+    for step in range(n - 1):
+        filt_copy(rank, peer(step)).start()
+    mine = pl.ds(pl.multiple_of(rank * span, 128), span)
+    filt_recv[:, mine] = filt_ref[pl.ds(pl.multiple_of(rank * part, HALF), part), :]
+
+    def offsets_of(ahead, width):
+        position = rank * span + ahead + lax.broadcasted_iota(jnp.int32, (8, width), 1)
+        result = position
+        end = jnp.int32(0)
+        for g in range(lengths_ref.shape[0]):
+            one = lengths_ref[g]
+            end = end + one
+            result = result - jnp.where(end <= position, one, 0)
+        return result
+
+    off_wide = offsets_of(0, wide)
+    keep_s[0] = jnp.where(offsets_of(1, span) >= 1, 1.0, 0.0)
+    keep_s[1] = jnp.where(offsets_of(2, span) >= 2, 1.0, 0.0)
+    src_id = lax.broadcasted_iota(jnp.int32, (span, wide), 0)
+    dst_id = lax.broadcasted_iota(jnp.int32, (span, wide), 1)
+    row_id = lax.broadcasted_iota(jnp.int32, (32, wide), 0)
+    col_id = lax.broadcasted_iota(jnp.int32, (32, wide), 1)
+    for j in range(3):
+        keep = jnp.where(off_wide >= j, 1.0, 0.0)[0:1, :]
+        shift_m[j] = (jnp.where(dst_id - j == src_id, 1.0, 0.0) * keep).astype(bf)
+        for a in range(4):
+            hit = (
+                ((row_id == 4 * a) & (col_id - j == -2)) | ((row_id == 4 * a + 1) & (col_id - j == -1))
+                | ((row_id == 16 + 4 * a + 2) & (col_id - j == span))
+                | ((row_id == 16 + 4 * a + 3) & (col_id - j == span + 1))
+            )
+            place[a, j] = (jnp.where(hit, 1.0, 0.0) * keep).astype(bf)
+
+    @pl.when(rank > 0)
+    def _():
+        rim_copy(0, rank).wait_recv()
+
+    @pl.when(rank < n - 1)
+    def _():
+        rim_copy(1, rank).wait_recv()
+
+    def prepare(index, carry):
+        sub = index // n
+        dest = lax.rem(rank + 1 + lax.rem(index, n), n)
+        first = pl.multiple_of(dest * part + sub * HALF, HALF)
+        rows = pl.ds(first, HALF)
+        rim_part = rim[:, rows]
+        par = par_ref[rows, :]
+
+        def shifted_in(a, j):
+            source = feat_ref[a, rows, :] if a < 3 else dout_ref[rows, :]
+            return mm(source, shift_m[j]) + mm(rim_part, place[a, j], TN)
+
+        result = []
+        for a in range(3):
+            acc = par[:, 3 * a : 3 * a + 1] * shifted_in(a, 0)
+            acc = acc + par[:, 3 * a + 1 : 3 * a + 2] * shifted_in(a, 1)
+            acc = acc + par[:, 3 * a + 2 : 3 * a + 3] * shifted_in(a, 2)
+            result.append(acc.astype(bf))
+        d_wide = shifted_in(3, 0).astype(bf)
+        q_s[rows, :] = result[0][:, :span]
+        k_s[rows, :] = result[1]
+        v_s[rows, :] = result[2]
+        d_s[rows, :] = d_wide
+        mixed = (result[1][:, :span].astype(f32) * result[2][:, :span].astype(f32)).astype(bf)
+        grad_in = (d_wide[:, :span].astype(f32) * result[0][:, :span].astype(f32)).astype(bf)
+
+        @pl.when(dest != rank)
+        def _():
+            fwd_send[sub, dest, 0:HALF, :] = mixed
+            fwd_send[sub, dest, HALF:, :] = grad_in
+            fwd_copy(sub, rank, dest).start()
+
+        @pl.when(dest == rank)
+        def _():
+            fwd_recv[sub, 0:HALF, mine] = mixed
+            fwd_recv[sub, HALF:, mine] = grad_in
+
+        return carry
+
+    lax.fori_loop(0, n * subs, prepare, 0)
+
+    fine_c = tab_ref[2]
+    fine_s = tab_ref[3]
+
+    def build(a, carry):
+        big_c = tab_ref[0, pl.ds(a, 1), :]
+        big_s = tab_ref[1, pl.ds(a, 1), :]
+        rows = pl.ds(pl.multiple_of(a * FINE, FINE), FINE)
+        table[rows, 0:length] = (big_c * fine_c - big_s * fine_s).astype(bf)
+        table[rows, length:] = (big_s * fine_c + big_c * fine_s).astype(bf)
+        return carry
+
+    lax.fori_loop(0, length // FINE, build, 0)
+
+    for step in range(n - 1):
+        filt_copy(peer(step), rank).wait_recv()
+
+    tile = 256
+
+    def filter_tile(t, carry):
+        cols = pl.ds(pl.multiple_of(t * tile, tile), tile)
+        spec_h[:, cols] = mm(filt_recv[...], table[:, cols])
+        return carry
+
+    lax.fori_loop(0, 2 * length // tile, filter_tile, 0)
+
+    for sub in range(subs):
+        for step in range(n - 1):
+            fwd_copy(sub, peer(step), rank).wait_recv()
+        h_rows = pl.ds(sub * HALF, HALF)
+
+        def spectrum_tile(t, carry):
+            cols = pl.ds(pl.multiple_of(t * tile, tile), tile)
+            sins = pl.ds(pl.multiple_of(length + t * tile, tile), tile)
+            signal = fwd_recv[sub]
+            x_c = mm(signal, table[:, cols])
+            x_s = mm(signal, table[:, sins])
+            h_c = spec_h[h_rows, cols]
+            h_s = spec_h[h_rows, sins]
+            spec[0:HALF, cols] = (h_c * x_c[:HALF] - h_s * x_s[:HALF]).astype(bf)
+            spec[0:HALF, sins] = (h_c * x_s[:HALF] + h_s * x_c[:HALF]).astype(bf)
+            spec[HALF:, cols] = (h_c * x_c[HALF:] + h_s * x_s[HALF:]).astype(bf)
+            spec[HALF:, sins] = (h_c * x_s[HALF:] - h_s * x_c[HALF:]).astype(bf)
+            return carry
+
+        lax.fori_loop(0, length // tile, spectrum_tile, 0)
+        skip_col = par_ref[pl.ds(pl.multiple_of(rank * part + sub * HALF, HALF), HALF), 9:10]
+
+        def give_back(step, carry):
+            dest = lax.rem(rank + 1 + step, n)
+            block = pl.ds(pl.multiple_of(dest * span, 128), span)
+            value = mm(spec[...], table[block, :], NT) * (1.0 / length)
+            signal = fwd_recv[sub, :, block].astype(f32)
+            y_part = (value[:HALF] + skip_col * signal[:HALF]).astype(bf)
+            d_part = (value[HALF:] + skip_col * signal[HALF:]).astype(bf)
+
+            @pl.when(dest != rank)
+            def _():
+                y_send[sub, dest, 0:HALF, :] = y_part
+                y_send[sub, dest, HALF:, :] = d_part
+                y_copy(sub, rank, dest).start()
+
+            @pl.when(dest == rank)
+            def _():
+                y_recv[sub, rank, 0:HALF, :] = y_part
+                y_recv[sub, rank, HALF:, :] = d_part
+
+            return carry
+
+        lax.fori_loop(0, n, give_back, 0)
+
+    r_id = lax.broadcasted_iota(jnp.int32, (16, 128), 0)
+    c_id = lax.broadcasted_iota(jnp.int32, (16, 128), 1)
+    eye = jnp.where((r_id == c_id) & (r_id < 2), 1.0, 0.0).astype(bf)
+
+    def halo_send(sub):
+        for step in range(n - 1):
+            y_copy(sub, peer(step), rank).wait_recv()
+        for s in range(n):
+            hal_src[sub, :, s * 2 * HALF : (s + 1) * 2 * HALF] = mm(eye, y_recv[sub, s, :, 0:128], NT).astype(bf)
+
+        @pl.when(rank > 0)
+        def _():
+            hal_copy(sub, rank - 1).start()
+
+    def finish(sub):
+        @pl.when(rank < n - 1)
+        def _():
+            hal_copy(sub, rank).wait_recv()
+
+        def rows_of(s, carry):
+            rows = pl.ds(pl.multiple_of(s * part + sub * HALF, HALF), HALF)
+            par = par_ref[rows, :]
+            y_rim = mm(hal[sub, :, pl.ds(pl.multiple_of(s * 2 * HALF, HALF), HALF)], eye, TN)
+            d_rim = mm(hal[sub, :, pl.ds(pl.multiple_of(s * 2 * HALF + HALF, HALF), HALF)], eye, TN)
+            y_here = y_recv[sub, s, 0:HALF, :].astype(f32)
+            d_here = y_recv[sub, s, HALF:, :].astype(f32)
+            out_ref[rows, :] = (q_s[rows, :].astype(f32) * y_here).astype(bf)
+            y_wide = jnp.concatenate([y_here, y_rim], axis=1)
+            d_wide = jnp.concatenate([d_here, d_rim], axis=1)
+            for c in range(3):
+                if c == 0:
+                    grads = d_s[rows, :].astype(f32) * y_wide
+                elif c == 1:
+                    grads = d_wide * v_s[rows, :].astype(f32)
+                else:
+                    grads = d_wide * k_s[rows, :].astype(f32)
+                acc = par[:, 3 * c : 3 * c + 1] * grads[:, :span]
+                for j in (1, 2):
+                    moved = pltpu.roll(grads, wide - j, 1)[:, :span]
+                    acc = acc + par[:, 3 * c + j : 3 * c + j + 1] * moved * keep_s[j - 1, 0:1, :]
+                df_ref[c, rows, :] = acc.astype(bf)
+            return carry
+
+        lax.fori_loop(0, n, rows_of, 0)
+
+    for sub in range(subs):
+        halo_send(sub)
+        if sub > 0:
+            finish(sub - 1)
+    finish(subs - 1)
+
+    @pl.when(rank < n - 1)
+    def _():
+        rim_copy(0, rank).wait_send()
+
+    @pl.when(rank > 0)
+    def _():
+        rim_copy(1, rank).wait_send()
+        for sub in range(subs):
+            hal_copy(sub, rank).wait_send()
+
+    for step in range(n - 1):
+        filt_copy(rank, peer(step)).wait_send()
+        for sub in range(subs):
+            fwd_copy(sub, rank, peer(step)).wait_send()
+            y_copy(sub, rank, peer(step)).wait_send()
+
+
+def local_kernel(features, dout, filters, taps, skip, lengths):
+    n = lax.axis_size("seq")
+    channels, span = dout.shape
+    part = channels // n
+    subs = part // HALF
+    length = n * span
+    wide = span + 128
+    bf = jnp.bfloat16
+    par = jnp.concatenate([taps.reshape(9, channels), skip[None]], axis=0).T
+    tab = jnp.asarray(np.stack(angle_parts(length)))
+    vmem = pl.BlockSpec(memory_space=pltpu.VMEM)
+    dma = pltpu.SemaphoreType.DMA
+    return pl.pallas_call(
+        functools.partial(mixer_kernel, n),
+        out_shape=(
+            jax.ShapeDtypeStruct(dout.shape, bf),
+            jax.ShapeDtypeStruct(features.shape, bf),
+        ),
+        in_specs=[pl.BlockSpec(memory_space=pltpu.SMEM)] + [vmem] * 5,
+        out_specs=(vmem, vmem),
+        scratch_shapes=[
+            pltpu.VMEM((16, channels), bf),
+            pltpu.VMEM((32, channels), bf),
+            pltpu.VMEM((3, span, wide), bf),
+            pltpu.VMEM((4, 3, 32, wide), bf),
+            pltpu.VMEM((2, 8, span), jnp.float32),
+            pltpu.VMEM((channels, span), bf),
+            pltpu.VMEM((channels, wide), bf),
+            pltpu.VMEM((channels, wide), bf),
+            pltpu.VMEM((channels, wide), bf),
+            pltpu.VMEM((subs, n, 2 * HALF, span), bf),
+            pltpu.VMEM((subs, 2 * HALF, length), bf),
+            pltpu.VMEM((part, length), bf),
+            pltpu.VMEM((length, 2 * length), bf),
+            pltpu.VMEM((part, 2 * length), jnp.float32),
+            pltpu.VMEM((2 * HALF, 2 * length), bf),
+            pltpu.VMEM((subs, n, 2 * HALF, span), bf),
+            pltpu.VMEM((subs, n, 2 * HALF, span), bf),
+            pltpu.VMEM((subs, 16, n * 2 * HALF), bf),
+            pltpu.VMEM((subs, 16, n * 2 * HALF), bf),
+            dma((2,)), dma((2,)),
+            dma((n,)), dma((n,)),
+            dma((subs, n)), dma((subs, n)),
+            dma((subs, n)), dma((subs, n)),
+            dma((subs,)), dma((subs,)),
+        ],
+        compiler_params=pltpu.CompilerParams(
+            collective_id=0, has_side_effects=True, vmem_limit_bytes=56 * 1024 * 1024
+        ),
+    )(lengths, features, dout, filters, par, tab)
+
+
+def local(features, dout, filters, taps, skip, lengths):
+    blocks = lax.axis_size("seq")
+    channels, span = dout.shape
+    fits = blocks * span <= DENSE_MAX and taps.shape[1] == 3
+    if fits and span % 128 == 0 and channels % (blocks * HALF) == 0:
+        return local_kernel(features, dout, filters, taps, skip, lengths)
+    return local_general(features, dout, filters, taps, skip, lengths)
+
+
 def solution(mesh):
     in_specs = (
         P(None, ("chan", "sub"), ("groups", "seq")),

time: 134 us -> 80.8 us (0.60)
  waiting for transfers between devices: 73.1 us -> 0 us
  Pallas kernels: 0 us -> 72.8 us
  other arithmetic: 18.5 us -> 0.7 us
  starting transfers between devices: 14.1 us -> 0 us
  local copies, waits for them, and re-layouts: 20 us -> 6.36 us
  matrix products: 6.44 us -> 0 us
    pallas_call x0 -> x1, Pallas kernels: none -> 72.8 us  [local_kernel(): pl.pallas_call(functools.partial(mixer_kernel, n), out_shape=(jax.ShapeDt...]
    all_to_all x2 -> x0, waiting for transfers between devices: 68.7 us -> none  [the longest x1 43.4 us: to_channels(): lax.all_to_all(stacked, 'seq', split_axis=1, concat_axis=2, tiled=True)]
    all_to_all x2 -> x0, starting transfers between devices: 7.82 us -> none  [the longest x1 4.31 us: to_channels(): lax.all_to_all(stacked, 'seq', split_axis=1, concat_axis=2, tiled=True)]
    another operation x9 -> x0, other arithmetic: 7.26 us -> none
    convert_element_type x5 -> x0, other arithmetic: 7.18 us -> none  [the longest x1 3.92 us: local(): short_backward(grads_ext, taps, offsets_ext).astype(jnp.bfloat16)]
    dot_general x5 -> x0, matrix products: 6.44 us -> none  [the longest x3 3.81 us: fwd(): return jnp.dot(x, table, preferred_element_type=jnp.float32)]
    slice x6 -> x0, local copies, waits for them, and re-layouts: 6.36 us -> none  [the longest x2 3.27 us: local(): ahead = shifted(grads[:, :, :margin], 'seq', -1)]
    ppermute x2 -> x0, starting transfers between devices: 6.25 us -> none  [shifted(): lax.ppermute(value, axis, [(source, source + steps) for source in range(l...]
  transfers between devices with their start and end apart: 4 -> 0, of which waited for: 3 -> 0; matrix products, arithmetic and copies ran while one was open for 5% -> 0% of each run, Pallas kernels for 0% -> 0%
where the time goes in v2:
time: 80.8 us; the launch traced here: 80.5 us
  Pallas kernels  72.8 us (90%)
  local copies, waits for them, and re-layouts  6.36 us (8%)
    pallas_call x1, Pallas kernels, local_kernel(): pl.pallas_call(functools.partial(mixer_kernel, n), out_shape=(jax.ShapeDt...  72.8 us
    unnamed x2, local copies, waits for them, and re-layouts  4.52 us

profile of v2, /device:TPU:0, one launch (start us, length us, event | category | flops | bytes accessed | tf_op | source)
XLA Modules:
  0.0 80.5 jit_solution(16663545712082372217)
XLA Ops:
  0.6 0.8 %reshape.7 = f32[9,1024]{1,0:T(8,128)S(1)} reshape(f32[3,3,1024]{2,1,0:T(4,128)} %param.10) | data formatting | bytes 73728 | tf_op jit(solution)/shard_map/reshape | solution.py:522
  1.5 0.7 pad_maximum_fusion
  2.2 1.0 %copy.12 = f32[10,1024]{0,1:T(8,128)} copy(f32[10,1024]{1,0:T(8,128)S(1)} %pad_maximum_fusion) | data formatting | bytes 81920 | tf_op jit(solution)/shard_map/concatenate | solution.py:522
  3.2 72.8 %shard_map.86 = (bf16[1024,256]{1,0:T(8,128)(2,1)}, bf16[3,1024,256]{2,1,0:T(8,128)(2,1)}) custom-call(s32[16]{0:T(128)} %lengths_ref.1, bf16[3,1024,256]{2,1,0:T(8,128)(2,1)} %feat_ref.1, bf16[1024,256]{1,0:T(8,128)(2,1)} %dout_ref.1, bf16[1024,256]{1,0:T(8,128)(2,1)} %filt_ref.1, f32[1024,10]{1,0:T(8,128)} %bitcast.2, f32[4,32,1024]{2,1,0:T(8,128)} %constant.2.clone.tab_ref), custom_call_target="tpu_custom_call" | custom-call | tf_op jit(solution)/shard_map/pallas_call | solution.py:526
  75.9 1.9 %copy.15 = bf16[1024,256]{1,0:T(8,128)(2,1)} copy(bf16[1024,256]{1,0:T(8,128)(2,1)} %get-tuple-element.4) | data formatting | bytes 1048576
  77.8 2.7 %copy.16 = bf16[3,1024,256]{2,1,0:T(8,128)(2,1)} copy(bf16[3,1024,256]{2,1,0:T(8,128)(2,1)} %get-tuple-element.5) | data formatting | bytes 3145728

commit v3 on v2

--- a/solution.py
+++ b/solution.py
@@ -215,17 +215,28 @@
     lengths_ref, feat_ref, dout_ref, filt_ref, par_ref, tab_ref,
     out_ref, df_ref,
     rim_src, rim, shift_m, place, keep_s, q_s, k_s, v_s, d_s,
-    fwd_send, fwd_recv, filt_recv, table, spec_h, spec, y_send, y_recv, hal_src, hal,
-    rim_ss, rim_rs, filt_ss, filt_rs, fwd_ss, fwd_rs, y_ss, y_rs, hal_ss, hal_rs,
+    fwd_send, fwd_recv, table, spec, y_send, y_recv, hal_src, hal,
+    rim_ss, rim_rs, fwd_ss, fwd_rs, far_ss, far_rs, filt_ss, filt_rs, twin_ss, twin_rs,
+    y_ss, y_rs, hal_ss, hal_rs,
 ):
     rank = lax.axis_index("seq")
     span = feat_ref.shape[2]
-    part = feat_ref.shape[1] // n
-    subs = part // HALF
+    blocks = feat_ref.shape[1] // HALF
     length = span * n
+    half = length // 2
     wide = span + 128
     bf = jnp.bfloat16
     f32 = jnp.float32
+    group = lax.axis_index("groups")
+    side = rank // 2
+    inner = (rank == 1) | (rank == 2)
+    outer = (rank == 0) | (rank == 3)
+    middle = 1 + side
+    edge = 3 * side
+    across = 2 - side
+    near = pl.ds(pl.multiple_of(side * half, 128), half)
+    far = pl.ds(pl.multiple_of((1 - side) * half, 128), half)
+    mine = pl.ds(pl.multiple_of(rank * span, 128), span)
 
     def peer(step):
         return lax.rem(rank + 1 + step, n)
@@ -233,6 +244,7 @@
     barrier = pltpu.get_barrier_semaphore()
     for step in range(n - 1):
         pl.semaphore_signal(barrier, inc=1, device_id={"seq": peer(step)}, device_id_type=pl.DeviceIdType.MESH)
+    pl.semaphore_signal(barrier, inc=1, device_id={"groups": 1 - group}, device_id_type=pl.DeviceIdType.MESH)
 
     def remote(src, dst, ss, rs, dest):
         return pltpu.make_async_remote_copy(
@@ -243,20 +255,29 @@
     def rim_copy(side, dest):
         return remote(rim_src, rim.at[pl.ds(16 * side, 16)], rim_ss.at[side], rim_rs.at[side], dest)
 
-    def filt_copy(who, dest):
-        rows = pl.ds(pl.multiple_of(dest * part, HALF), part)
-        cols = pl.ds(pl.multiple_of(who * span, 128), span)
-        return remote(filt_ref.at[rows], filt_recv.at[:, cols], filt_ss.at[dest], filt_rs.at[who], dest)
-
-    def fwd_copy(sub, who, dest):
-        cols = pl.ds(pl.multiple_of(who * span, 128), span)
-        return remote(fwd_send.at[sub, dest], fwd_recv.at[sub, :, cols], fwd_ss.at[sub, dest], fwd_rs.at[sub, who], dest)
-
-    def y_copy(sub, who, dest):
-        return remote(y_send.at[sub, dest], y_recv.at[sub, who], y_ss.at[sub, dest], y_rs.at[sub, who], dest)
-
-    def hal_copy(sub, dest):
-        return remote(hal_src.at[sub], hal.at[sub], hal_ss.at[sub], hal_rs.at[sub], dest)
+    def fwd_copy(b):
+        return remote(fwd_send.at[b], fwd_recv.at[b, :, mine], fwd_ss.at[b], fwd_rs.at[b], middle)
+
+    def far_copy(b):
+        rows = pl.ds(pl.multiple_of(side * HALF, HALF), HALF)
+        return remote(fwd_recv.at[b, rows, near], fwd_recv.at[b, rows, near], far_ss.at[b], far_rs.at[b], across)
+
+    def filt_copy(b):
+        rows = pl.ds(2 * HALF, HALF)
+        return remote(fwd_recv.at[b, rows, near], fwd_recv.at[b, rows, near], filt_ss.at[b], filt_rs.at[b], across)
+
+    def twin_copy(b):
+        part = fwd_recv.at[b, pl.ds(2 * HALF, HALF), far]
+        return pltpu.make_async_remote_copy(
+            src_ref=part, dst_ref=part, send_sem=twin_ss.at[b], recv_sem=twin_rs.at[b],
+            device_id={"groups": 1 - group}, device_id_type=pl.DeviceIdType.MESH,
+        )
+
+    def y_copy(b):
+        return remote(y_send.at[b], y_recv.at[b], y_ss.at[b], y_rs.at[b], edge)
+
+    def hal_copy(b, dest):
+        return remote(hal_src.at[b], hal.at[b], hal_ss.at[b], hal_rs.at[b], dest)
 
     r_id = lax.broadcasted_iota(jnp.int32, (16, span), 0)
     p_id = lax.broadcasted_iota(jnp.int32, (16, span), 1)
@@ -278,10 +299,15 @@
     @pl.when(rank == n - 1)
     def _():
         rim[16:32, :] = jnp.zeros((16, rim.shape[1]), bf)
-        for sub in range(subs):
-            hal[sub] = jnp.zeros(hal.shape[1:], bf)
-
-    pl.semaphore_wait(barrier, n - 1)
+        hal[...] = jnp.zeros(hal.shape, bf)
+
+    @pl.when(inner)
+    def _():
+        rows = pl.ds(pl.multiple_of(side * HALF, HALF), HALF)
+        for b in range(blocks):
+            fwd_recv[b, rows, far] = jnp.zeros((HALF, half), bf)
+
+    pl.semaphore_wait(barrier, n)
 
     @pl.when(rank < n - 1)
     def _():
@@ -290,11 +316,6 @@
     @pl.when(rank > 0)
     def _():
         rim_copy(1, rank - 1).start()
-
-    for step in range(n - 1):
-        filt_copy(rank, peer(step)).start()
-    mine = pl.ds(pl.multiple_of(rank * span, 128), span)
-    filt_recv[:, mine] = filt_ref[pl.ds(pl.multiple_of(rank * part, HALF), part), :]
 
     def offsets_of(ahead, width):
         position = rank * span + ahead + lax.broadcasted_iota(jnp.int32, (8, width), 1)
@@ -332,11 +353,8 @@
     def _():
         rim_copy(1, rank).wait_recv()
 
-    def prepare(index, carry):
-        sub = index // n
-        dest = lax.rem(rank + 1 + lax.rem(index, n), n)
-        first = pl.multiple_of(dest * part + sub * HALF, HALF)
-        rows = pl.ds(first, HALF)
+    def prepare(b):
+        rows = pl.ds(pl.multiple_of(b * HALF, HALF), HALF)
         rim_part = rim[:, rows]
         par = par_ref[rows, :]
 
@@ -358,20 +376,37 @@
         mixed = (result[1][:, :span].astype(f32) * result[2][:, :span].astype(f32)).astype(bf)
         grad_in = (d_wide[:, :span].astype(f32) * result[0][:, :span].astype(f32)).astype(bf)
 
-        @pl.when(dest != rank)
-        def _():
-            fwd_send[sub, dest, 0:HALF, :] = mixed
-            fwd_send[sub, dest, HALF:, :] = grad_in
-            fwd_copy(sub, rank, dest).start()
-
-        @pl.when(dest == rank)
-        def _():
-            fwd_recv[sub, 0:HALF, mine] = mixed
-            fwd_recv[sub, HALF:, mine] = grad_in
-
-        return carry
-
-    lax.fori_loop(0, n * subs, prepare, 0)
+        @pl.when(outer)
+        def _():
+            fwd_send[b, 0:HALF, :] = mixed
+            fwd_send[b, HALF : 2 * HALF, :] = grad_in
+            fwd_send[b, 2 * HALF :, :] = filt_ref[rows, :]
+            fwd_copy(b).start()
+
+        @pl.when(inner)
+        def _():
+            fwd_recv[b, 0:HALF, mine] = mixed
+            fwd_recv[b, HALF : 2 * HALF, mine] = grad_in
+            fwd_recv[b, 2 * HALF :, mine] = filt_ref[rows, :]
+
+    def own(b):
+        return lax.rem(b, 2) == group
+
+    def relay(b):
+        fwd_copy(b).wait_recv()
+        far_copy(b).start()
+
+        @pl.when(own(b))
+        def _():
+            filt_copy(b).start()
+
+    def collect(b):
+        far_copy(b).wait_recv()
+
+        @pl.when(own(b))
+        def _():
+            filt_copy(b).wait_recv()
+            twin_copy(b).start()
 
     fine_c = tab_ref[2]
     fine_s = tab_ref[3]
@@ -384,91 +419,75 @@
         table[rows, length:] = (big_s * fine_c + big_c * fine_s).astype(bf)
         return carry
 
-    lax.fori_loop(0, length // FINE, build, 0)
-
-    for step in range(n - 1):
-        filt_copy(peer(step), rank).wait_recv()
-
     tile = 256
 
-    def filter_tile(t, carry):
-        cols = pl.ds(pl.multiple_of(t * tile, tile), tile)
-        spec_h[:, cols] = mm(filt_recv[...], table[:, cols])
-        return carry
-
-    lax.fori_loop(0, 2 * length // tile, filter_tile, 0)
-
-    for sub in range(subs):
-        for step in range(n - 1):
-            fwd_copy(sub, peer(step), rank).wait_recv()
-        h_rows = pl.ds(sub * HALF, HALF)
+    def transform(b):
+        @pl.when(jnp.logical_not(own(b)))
+        def _():
+            twin_copy(b).wait_recv()
 
         def spectrum_tile(t, carry):
             cols = pl.ds(pl.multiple_of(t * tile, tile), tile)
             sins = pl.ds(pl.multiple_of(length + t * tile, tile), tile)
-            signal = fwd_recv[sub]
+            signal = fwd_recv[b]
             x_c = mm(signal, table[:, cols])
             x_s = mm(signal, table[:, sins])
-            h_c = spec_h[h_rows, cols]
-            h_s = spec_h[h_rows, sins]
-            spec[0:HALF, cols] = (h_c * x_c[:HALF] - h_s * x_s[:HALF]).astype(bf)
-            spec[0:HALF, sins] = (h_c * x_s[:HALF] + h_s * x_c[:HALF]).astype(bf)
-            spec[HALF:, cols] = (h_c * x_c[HALF:] + h_s * x_s[HALF:]).astype(bf)
-            spec[HALF:, sins] = (h_c * x_s[HALF:] - h_s * x_c[HALF:]).astype(bf)
+            h_c = x_c[2 * HALF :]
+            h_s = x_s[2 * HALF :]
+            m_c, g_c = x_c[:HALF], x_c[HALF : 2 * HALF]
+            m_s, g_s = x_s[:HALF], x_s[HALF : 2 * HALF]
+            spec[0:HALF, cols] = (h_c * m_c - h_s * m_s).astype(bf)
+            spec[0:HALF, sins] = (h_c * m_s + h_s * m_c).astype(bf)
+            spec[HALF:, cols] = (h_c * g_c + h_s * g_s).astype(bf)
+            spec[HALF:, sins] = (h_c * g_s - h_s * g_c).astype(bf)
             return carry
 
         lax.fori_loop(0, length // tile, spectrum_tile, 0)
-        skip_col = par_ref[pl.ds(pl.multiple_of(rank * part + sub * HALF, HALF), HALF), 9:10]
-
-        def give_back(step, carry):
-            dest = lax.rem(rank + 1 + step, n)
-            block = pl.ds(pl.multiple_of(dest * span, 128), span)
-            value = mm(spec[...], table[block, :], NT) * (1.0 / length)
-            signal = fwd_recv[sub, :, block].astype(f32)
+        skip_col = par_ref[pl.ds(pl.multiple_of(b * HALF, HALF), HALF), 9:10]
+
+        def results(dest):
+            cols = pl.ds(pl.multiple_of(dest * span, 128), span)
+            value = mm(spec[...], table[cols, :], NT) * (1.0 / length)
+            signal = fwd_recv[b, 0 : 2 * HALF, cols].astype(f32)
             y_part = (value[:HALF] + skip_col * signal[:HALF]).astype(bf)
             d_part = (value[HALF:] + skip_col * signal[HALF:]).astype(bf)
-
-            @pl.when(dest != rank)
-            def _():
-                y_send[sub, dest, 0:HALF, :] = y_part
-                y_send[sub, dest, HALF:, :] = d_part
-                y_copy(sub, rank, dest).start()
-
-            @pl.when(dest == rank)
-            def _():
-                y_recv[sub, rank, 0:HALF, :] = y_part
-                y_recv[sub, rank, HALF:, :] = d_part
-
-            return carry
-
-        lax.fori_loop(0, n, give_back, 0)
+            return y_part, d_part
+
+        y_part, d_part = results(edge)
+        y_send[b, 0:HALF, :] = y_part
+        y_send[b, HALF:, :] = d_part
+        y_copy(b).start()
+        y_part, d_part = results(rank)
+        y_recv[b, 0:HALF, :] = y_part
+        y_recv[b, HALF:, :] = d_part
 
     r_id = lax.broadcasted_iota(jnp.int32, (16, 128), 0)
     c_id = lax.broadcasted_iota(jnp.int32, (16, 128), 1)
     eye = jnp.where((r_id == c_id) & (r_id < 2), 1.0, 0.0).astype(bf)
 
-    def halo_send(sub):
-        for step in range(n - 1):
-            y_copy(sub, peer(step), rank).wait_recv()
-        for s in range(n):
-            hal_src[sub, :, s * 2 * HALF : (s + 1) * 2 * HALF] = mm(eye, y_recv[sub, s, :, 0:128], NT).astype(bf)
+    def halo_send(b):
+        @pl.when(outer)
+        def _():
+            y_copy(b).wait_recv()
+
+        hal_src[b] = mm(eye, y_recv[b, :, 0:128], NT).astype(bf)
 
         @pl.when(rank > 0)
         def _():
-            hal_copy(sub, rank - 1).start()
-
-    def finish(sub):
+            hal_copy(b, rank - 1).start()
+
+    def finish(b):
         @pl.when(rank < n - 1)
         def _():
-            hal_copy(sub, rank).wait_recv()
-
-        def rows_of(s, carry):
-            rows = pl.ds(pl.multiple_of(s * part + sub * HALF, HALF), HALF)
+            hal_copy(b, rank).wait_recv()
+
+        if True:
+            rows = pl.ds(pl.multiple_of(b * HALF, HALF), HALF)
             par = par_ref[rows, :]
-            y_rim = mm(hal[sub, :, pl.ds(pl.multiple_of(s * 2 * HALF, HALF), HALF)], eye, TN)
-            d_rim = mm(hal[sub, :, pl.ds(pl.multiple_of(s * 2 * HALF + HALF, HALF), HALF)], eye, TN)
-            y_here = y_recv[sub, s, 0:HALF, :].astype(f32)
-            d_here = y_recv[sub, s, HALF:, :].astype(f32)
+            y_rim = mm(hal[b, :, 0:HALF], eye, TN)
+            d_rim = mm(hal[b, :, HALF:], eye, TN)
+            y_here = y_recv[b, 0:HALF, :].astype(f32)
+            d_here = y_recv[b, HALF:, :].astype(f32)
             out_ref[rows, :] = (q_s[rows, :].astype(f32) * y_here).astype(bf)
             y_wide = jnp.concatenate([y_here, y_rim], axis=1)
             d_wide = jnp.concatenate([d_here, d_rim], axis=1)
@@ -484,15 +503,30 @@
                     moved = pltpu.roll(grads, wide - j, 1)[:, :span]
                     acc = acc + par[:, 3 * c + j : 3 * c + j + 1] * moved * keep_s[j - 1, 0:1, :]
                 df_ref[c, rows, :] = acc.astype(bf)
-            return carry
-
-        lax.fori_loop(0, n, rows_of, 0)
-
-    for sub in range(subs):
-        halo_send(sub)
-        if sub > 0:
-            finish(sub - 1)
-    finish(subs - 1)
+
+    def at(step, lag, work, only=None):
+        b = step - lag
+        ready = (b >= 0) & (b < blocks)
+
+        @pl.when(ready if only is None else ready & only)
+        def _():
+            work(b)
+
+    def advance(step, carry):
+        at(step, 0, prepare)
+        at(step, 1, relay, inner)
+        at(step, 4, collect, inner)
+        at(step, 5, transform, inner)
+        at(step, 6, halo_send)
+        at(step, 7, finish)
+
+        @pl.when(step == 2)
+        def _():
+            lax.fori_loop(0, length // FINE, build, 0)
+
+        return carry
+
+    lax.fori_loop(0, blocks + 7, advance, 0)
 
     @pl.when(rank < n - 1)
     def _():
@@ -501,21 +535,35 @@
     @pl.when(rank > 0)
     def _():
         rim_copy(1, rank).wait_send()
-        for sub in range(subs):
-            hal_copy(sub, rank).wait_send()
-
-    for step in range(n - 1):
-        filt_copy(rank, peer(step)).wait_send()
-        for sub in range(subs):
-            fwd_copy(sub, rank, peer(step)).wait_send()
-            y_copy(sub, rank, peer(step)).wait_send()
+
+    def drain(b, carry):
+        @pl.when(rank > 0)
+        def _():
+            hal_copy(b, rank).wait_send()
+
+        @pl.when(outer)
+        def _():
+            fwd_copy(b).wait_send()
+
+        @pl.when(inner)
+        def _():
+            far_copy(b).wait_send()
+            y_copy(b).wait_send()
+
+        @pl.when(inner & own(b))
+        def _():
+            filt_copy(b).wait_send()
+            twin_copy(b).wait_send()
+
+        return carry
+
+    lax.fori_loop(0, blocks, drain, 0)
 
 
 def local_kernel(features, dout, filters, taps, skip, lengths):
     n = lax.axis_size("seq")
     channels, span = dout.shape
-    part = channels // n
-    subs = part // HALF
+    blocks = channels // HALF
     length = n * span
     wide = span + 128
     bf = jnp.bfloat16
@@ -541,21 +589,21 @@
             pltpu.VMEM((channels, wide), bf),
             pltpu.VMEM((channels, wide), bf),
             pltpu.VMEM((channels, wide), bf),
-            pltpu.VMEM((subs, n, 2 * HALF, span), bf),
-            pltpu.VMEM((subs, 2 * HALF, length), bf),
-            pltpu.VMEM((part, length), bf),
+            pltpu.VMEM((blocks, 3 * HALF, span), bf),
+            pltpu.VMEM((blocks, 3 * HALF, length), bf),
             pltpu.VMEM((length, 2 * length), bf),
-            pltpu.VMEM((part, 2 * length), jnp.float32),
             pltpu.VMEM((2 * HALF, 2 * length), bf),
-            pltpu.VMEM((subs, n, 2 * HALF, span), bf),
-            pltpu.VMEM((subs, n, 2 * HALF, span), bf),
-            pltpu.VMEM((subs, 16, n * 2 * HALF), bf),
-            pltpu.VMEM((subs, 16, n * 2 * HALF), bf),
+            pltpu.VMEM((blocks, 2 * HALF, span), bf),
+            pltpu.VMEM((blocks, 2 * HALF, span), bf),
+            pltpu.VMEM((blocks, 16, 2 * HALF), bf),
+            pltpu.VMEM((blocks, 16, 2 * HALF), bf),
             dma((2,)), dma((2,)),
-            dma((n,)), dma((n,)),
-            dma((subs, n)), dma((subs, n)),
-            dma((subs, n)), dma((subs, n)),
-            dma((subs,)), dma((subs,)),
+            dma((blocks,)), dma((blocks,)),
+            dma((blocks,)), dma((blocks,)),
+            dma((blocks,)), dma((blocks,)),
+            dma((blocks,)), dma((blocks,)),
+            dma((blocks,)), dma((blocks,)),
+            dma((blocks,)), dma((blocks,)),
         ],
         compiler_params=pltpu.CompilerParams(
             collective_id=0, has_side_effects=True, vmem_limit_bytes=56 * 1024 * 1024
@@ -566,8 +614,8 @@
 def local(features, dout, filters, taps, skip, lengths):
     blocks = lax.axis_size("seq")
     channels, span = dout.shape
-    fits = blocks * span <= DENSE_MAX and taps.shape[1] == 3
-    if fits and span % 128 == 0 and channels % (blocks * HALF) == 0:
+    fits = blocks == 4 and lax.axis_size("groups") == 2 and blocks * span <= DENSE_MAX and taps.shape[1] == 3
+    if fits and span % 128 == 0 and channels % HALF == 0:
         return local_kernel(features, dout, filters, taps, skip, lengths)
     return local_general(features, dout, filters, taps, skip, lengths)
 

time: 80.8 us -> 87.2 us (1.079)
  Pallas kernels: 72.8 us -> 79.2 us
    pallas_call x1, Pallas kernels: 72.8 us -> 79.2 us  [local_kernel(): pl.pallas_call(functools.partial(mixer_kernel, n), out_shape=(jax.ShapeDt...]
where the time goes in v3:
time: 87.2 us; the launch traced here: 86.9 us
  Pallas kernels  79.2 us (91%)
  local copies, waits for them, and re-layouts  6.36 us (7%)
    pallas_call x1, Pallas kernels, local_kernel(): pl.pallas_call(functools.partial(mixer_kernel, n), out_shape=(jax.ShapeDt...  79.2 us
    unnamed x2, local copies, waits for them, and re-layouts  4.52 us

profile of v3, /device:TPU:0, one launch (start us, length us, event | category | flops | bytes accessed | tf_op | source)
XLA Modules:
  0.0 86.9 jit_solution(1540767784002817371)
XLA Ops:
  0.6 0.8 reshape.7
  1.5 0.7 pad_maximum_fusion
  2.2 1.0 %copy.12 = f32[10,1024]{0,1:T(8,128)} copy(f32[10,1024]{1,0:T(8,128)S(1)} %pad_maximum_fusion) | data formatting | bytes 81920 | tf_op jit(solution)/shard_map/concatenate | solution.py:570
  3.2 79.2 %shard_map.86 = (bf16[1024,256]{1,0:T(8,128)(2,1)}, bf16[3,1024,256]{2,1,0:T(8,128)(2,1)}) custom-call(s32[16]{0:T(128)} %lengths_ref.1, bf16[3,1024,256]{2,1,0:T(8,128)(2,1)} %feat_ref.1, bf16[1024,256]{1,0:T(8,128)(2,1)} %dout_ref.1, bf16[1024,256]{1,0:T(8,128)(2,1)} %filt_ref.1, f32[1024,10]{1,0:T(8,128)} %bitcast.2, f32[4,32,1024]{2,1,0:T(8,128)} %constant.2.clone.tab_ref), custom_call_target="tpu_custom_call" | custom-call | tf_op jit(solution)/shard_map/pallas_call | solution.py:574
  82.4 1.9 %copy.15 = bf16[1024,256]{1,0:T(8,128)(2,1)} copy(bf16[1024,256]{1,0:T(8,128)(2,1)} %get-tuple-element.4) | data formatting | bytes 1048576
  84.3 2.7 %copy.16 = bf16[3,1024,256]{2,1,0:T(8,128)(2,1)} copy(bf16[3,1024,256]{2,1,0:T(8,128)(2,1)} %get-tuple-element.5) | data formatting | bytes 3145728

commit v4 on v3

--- a/solution.py
+++ b/solution.py
@@ -513,20 +513,20 @@
             work(b)
 
     def advance(step, carry):
+        at(step, 3, relay, inner)
         at(step, 0, prepare)
-        at(step, 1, relay, inner)
         at(step, 4, collect, inner)
         at(step, 5, transform, inner)
-        at(step, 6, halo_send)
-        at(step, 7, finish)
-
-        @pl.when(step == 2)
+        at(step, 5, halo_send)
+        at(step, 6, finish)
+
+        @pl.when((step == 2) & inner)
         def _():
             lax.fori_loop(0, length // FINE, build, 0)
 
         return carry
 
-    lax.fori_loop(0, blocks + 7, advance, 0)
+    lax.fori_loop(0, blocks + 6, advance, 0)
 
     @pl.when(rank < n - 1)
     def _():

time: 87.2 us -> 86.3 us (0.990)
  Pallas kernels: 79.2 us -> 77.6 us
    pallas_call x1, Pallas kernels: 79.2 us -> 77.6 us  [local_kernel(): pl.pallas_call(functools.partial(mixer_kernel, n), out_shape=(jax.ShapeDt...]
where the time goes in v4:
time: 86.3 us; the launch traced here: 85.3 us
  Pallas kernels  77.6 us (90%)
  local copies, waits for them, and re-layouts  6.36 us (7%)
    pallas_call x1, Pallas kernels, local_kernel(): pl.pallas_call(functools.partial(mixer_kernel, n), out_shape=(jax.ShapeDt...  77.6 us
    unnamed x2, local copies, waits for them, and re-layouts  4.52 us

profile of v4, /device:TPU:0, one launch (start us, length us, event | category | flops | bytes accessed | tf_op | source)
XLA Modules:
  0.0 85.3 jit_solution(2080475779332807065)
XLA Ops:
  0.6 0.8 reshape.7
  1.5 0.7 pad_maximum_fusion
  2.2 1.0 %copy.12 = f32[10,1024]{0,1:T(8,128)} copy(f32[10,1024]{1,0:T(8,128)S(1)} %pad_maximum_fusion) | data formatting | bytes 81920 | tf_op jit(solution)/shard_map/concatenate | solution.py:570
  3.2 77.6 %shard_map.86 = (bf16[1024,256]{1,0:T(8,128)(2,1)}, bf16[3,1024,256]{2,1,0:T(8,128)(2,1)}) custom-call(s32[16]{0:T(128)} %lengths_ref.1, bf16[3,1024,256]{2,1,0:T(8,128)(2,1)} %feat_ref.1, bf16[1024,256]{1,0:T(8,128)(2,1)} %dout_ref.1, bf16[1024,256]{1,0:T(8,128)(2,1)} %filt_ref.1, f32[1024,10]{1,0:T(8,128)} %bitcast.2, f32[4,32,1024]{2,1,0:T(8,128)} %constant.2.clone.tab_ref), custom_call_target="tpu_custom_call" | custom-call | tf_op jit(solution)/shard_map/pallas_call | solution.py:574
  80.8 1.9 %copy.15 = bf16[1024,256]{1,0:T(8,128)(2,1)} copy(bf16[1024,256]{1,0:T(8,128)(2,1)} %get-tuple-element.4) | data formatting | bytes 1048576
  82.6 2.7 %copy.16 = bf16[3,1024,256]{2,1,0:T(8,128)(2,1)} copy(bf16[3,1024,256]{2,1,0:T(8,128)(2,1)} %get-tuple-element.5) | data formatting | bytes 3145728

commit v5 on v4

--- a/solution.py
+++ b/solution.py
@@ -200,7 +200,7 @@
     return (out, dfeatures)
 
 
-HALF = 128
+HALF = 256
 NN = (((1,), (0,)), ((), ()))
 NT = (((1,), (1,)), ((), ()))
 TN = (((0,), (0,)), ((), ()))
@@ -513,20 +513,20 @@
             work(b)
 
     def advance(step, carry):
-        at(step, 3, relay, inner)
+        at(step, 2, relay, inner)
         at(step, 0, prepare)
-        at(step, 4, collect, inner)
-        at(step, 5, transform, inner)
-        at(step, 5, halo_send)
-        at(step, 6, finish)
-
-        @pl.when((step == 2) & inner)
+        at(step, 3, collect, inner)
+        at(step, 3, transform, inner)
+        at(step, 3, halo_send)
+        at(step, 4, finish)
+
+        @pl.when((step == 1) & inner)
         def _():
             lax.fori_loop(0, length // FINE, build, 0)
 
         return carry
 
-    lax.fori_loop(0, blocks + 6, advance, 0)
+    lax.fori_loop(0, blocks + 4, advance, 0)
 
     @pl.when(rank < n - 1)
     def _():

time: 86.3 us -> 102 us (1.18)
  Pallas kernels: 77.6 us -> 94.1 us
    pallas_call x1, Pallas kernels: 77.6 us -> 94.1 us  [local_kernel(): pl.pallas_call(functools.partial(mixer_kernel, n), out_shape=(jax.ShapeDt...]
where the time goes in v5:
time: 102 us
  Pallas kernels  94.1 us (92%)
  local copies, waits for them, and re-layouts  6.36 us (6%)
    pallas_call x1, Pallas kernels, local_kernel(): pl.pallas_call(functools.partial(mixer_kernel, n), out_shape=(jax.ShapeDt...  94.1 us
    unnamed x2, local copies, waits for them, and re-layouts  4.52 us

profile of v5, /device:TPU:0, one launch (start us, length us, event | category | flops | bytes accessed | tf_op | source)
XLA Modules:
  0.0 101.8 jit_solution(12383955242439697354)
XLA Ops:
  0.6 0.8 reshape.7
  1.5 0.7 pad_maximum_fusion
  2.2 1.0 %copy.12 = f32[10,1024]{0,1:T(8,128)} copy(f32[10,1024]{1,0:T(8,128)S(1)} %pad_maximum_fusion) | data formatting | bytes 81920 | tf_op jit(solution)/shard_map/concatenate | solution.py:570
  3.2 94.1 %shard_map.86 = (bf16[1024,256]{1,0:T(8,128)(2,1)}, bf16[3,1024,256]{2,1,0:T(8,128)(2,1)}) custom-call(s32[16]{0:T(128)} %lengths_ref.1, bf16[3,1024,256]{2,1,0:T(8,128)(2,1)} %feat_ref.1, bf16[1024,256]{1,0:T(8,128)(2,1)} %dout_ref.1, bf16[1024,256]{1,0:T(8,128)(2,1)} %filt_ref.1, f32[1024,10]{1,0:T(8,128)} %bitcast.2, f32[4,32,1024]{2,1,0:T(8,128)} %constant.2.clone.tab_ref), custom_call_target="tpu_custom_call" | custom-call | tf_op jit(solution)/shard_map/pallas_call | solution.py:574
  97.3 1.9 %copy.15 = bf16[1024,256]{1,0:T(8,128)(2,1)} copy(bf16[1024,256]{1,0:T(8,128)(2,1)} %get-tuple-element.4) | data formatting | bytes 1048576
  99.1 2.7 %copy.16 = bf16[3,1024,256]{2,1,0:T(8,128)(2,1)} copy(bf16[3,1024,256]{2,1,0:T(8,128)(2,1)} %get-tuple-element.5) | data formatting | bytes 3145728
